TPU v7x, 128 devices: a whole 4x4x4 slice. The times are simulated.
128 devices in a mesh: dp: 8 (over y, core), seq: 16 (over x, z).
Axes of the slice: x: 4, y: 4, z: 4, core: 2. Of those that a mesh axis runs over, the one named last changes fastest.
Arguments:
- ssm_input: bfloat16 [8, 4096, 2048], P('dp', 'seq'), may hold values from -6 to 6
- write_basis: bfloat16 [8, 4096, 128], P('dp', 'seq'), may hold values from -2 to 2
- read_basis: bfloat16 [8, 4096, 128], P('dp', 'seq'), may hold values from -2 to 2
- step_size: float32 [8, 4096, 64], P('dp', 'seq')
- log_decay: float32 [8, 4096, 64], P('dp', 'seq')
- head_weight: bfloat16 [2048, 256], replicated, may hold values from -0.125 to 0.125
- block_list: int32 [8, 1024, 16], P('dp', 'seq'), may hold values from 0 to 4095, as said below
- block_count: int32 [8, 1024], P('dp', 'seq'), may hold values from 1 to 16, as said below
- depth_order: int32 [8, 1024, 16], P('dp', 'seq'), may hold values from 0 to 15, each once within a row
- camera_index: int32 [8, 1024], P('dp', 'seq'), may hold values from 0 to 7
- view_gain: float32 [8, 8, 3], P('dp'), may hold values from 0.1 to 1.9
- target_color: float32 [8, 1024, 192], P('dp', 'seq'), may hold values from 0 to 1
Outputs:
- input_grad: bfloat16 [8, 4096, 2048], P('dp', 'seq')
- weight_grad: float32 [2048, 256], replicated
Inputs may be any that keep to these rules, and one draw needn't show every extreme that they name: Each scene has a tile whose list holds 16 live slots; slots at block_count or beyond are unused. `depth_order`: each row is a permutation of 0 to 15. `block_list`: entries name tokens of the same scene. Of the 1024 slots of one aligned block of 64 tiles, used or not, at most 128 name tokens of any one aligned block of 256 tokens, and exactly 128 name tokens of some such block.
All inputs are finite; a program needn't handle non-finite values.
Results may differ from a plain program's by a relative error of at most 0.0085.
Values may be sent and summed in bfloat16 or wider, within the bound.
No kernel may reach another device: no remote copies, remote signals or barrier semaphores. Data moves between devices by JAX's collectives and lax.ppermute only.
A program may use at most 128 MiB of HBM per device.

v0:
```python
import jax
import jax.numpy as jnp
import numpy as np
from jax import lax
from jax.experimental import pallas as pl
from jax.experimental.pallas import tpu as pltpu
from jax.sharding import Mesh
from jax.sharding import PartitionSpec as P

SEQ = ("seq_0", "seq_1")
F32 = jnp.float32
BF16 = jnp.bfloat16
NEG = -1e30
LOG2E = 1.4426950408889634

OWN = 16
TOK = 256
BLK = 128
NST = 128
HEADS = 64
WID = 2048
FEAT = 256
CH = 256
NCH = WID // CH
TILES = 64
SLOTS = 16
ROWS = TILES * SLOTS
TAIL = 16


def dot(a, b):
    return lax.dot_general(a, b, (((1,), (0,)), ((), ())), preferred_element_type=F32)


def dot_t(a, b):
    return lax.dot_general(a, b, (((1,), (1,)), ((), ())), preferred_element_type=F32)


def iota(shape, dim):
    return lax.broadcasted_iota(jnp.int32, shape, dim)


def turned(a):
    return a.astype(F32).T.astype(BF16)


def split_pair(f):
    high = f.astype(BF16).astype(F32)
    return jnp.where(iota(f.shape, 1) < HEADS, high, f - high).astype(BF16)


def spreader():
    return (iota((2 * HEADS, CH), 0) & (HEADS - 1)) - (iota((2 * HEADS, CH), 1) >> 5)


def spread_of(base, c):
    return (base == 8 * c).astype(F32).astype(BF16)


def cols(c):
    return slice(c * CH, (c + 1) * CH)


def call(body, outs, scratch=(), in_specs=None, out_specs=None, limit=32, flops=0, grid=None, alias=None):
    kwargs = {}
    if in_specs is not None:
        kwargs["in_specs"] = in_specs
    if out_specs is not None:
        kwargs["out_specs"] = out_specs
    if grid is not None:
        kwargs["grid"] = grid
    return pl.pallas_call(
        body,
        out_shape=[jax.ShapeDtypeStruct(s, d) for s, d in outs],
        scratch_shapes=list(scratch),
        compiler_params=pltpu.CompilerParams(vmem_limit_bytes=limit << 20),
        cost_estimate=pl.CostEstimate(flops=flops, transcendentals=0, bytes_accessed=4 << 20),
        input_output_aliases=alias or {},
        **kwargs,
    )


def local_end_body(x, wr, step, logd, pay, run_out, step_out):
    ld = jnp.concatenate([logd[...], logd[...]], axis=1)
    st = jnp.concatenate([step[...], step[...]], axis=1)
    row = iota((TOK, 2 * HEADS), 0)
    run = ld
    s = 1
    while s < TOK:
        run = run + jnp.where(row >= s, pltpu.roll(run, s, 0), 0.0)
        s *= 2
    run_out[...] = run
    step_out[...] = st
    total = run[TOK - 1 : TOK, :]
    pair = split_pair(st * jnp.exp(total - run))
    t1 = total.astype(BF16).astype(F32)
    t2 = (total - t1).astype(BF16).astype(F32)
    t3 = total - t1 - t2
    trow = iota((TAIL, 2 * HEADS), 0)
    tails = jnp.where(trow == 0, t1, jnp.where(trow == 1, t2, jnp.where(trow == 2, t3, 0.0)))
    tails = jnp.where(iota((TAIL, 2 * HEADS), 1) < HEADS, tails, 0.0).astype(BF16)
    wt = turned(wr[...])
    base = spreader()
    for c in range(NCH):
        e = spread_of(base, c)
        xs = (x[:, cols(c)].astype(F32) * dot(pair, e)).astype(BF16)
        end = dot(wt, xs).astype(BF16)
        extra = dot(tails, e).astype(BF16)
        for k in range(2):
            lanes = slice(k * 128, (k + 1) * 128)
            pay[2 * c + k, 0:NST, :] = end[:, lanes]
            pay[2 * c + k, NST : NST + TAIL, :] = extra[:, lanes]


def decayed(tail):
    return jnp.exp(
        tail[0:1, :].astype(F32) + tail[1:2, :].astype(F32) + tail[2:3, :].astype(F32)
    )


def prefix_body(got, asks, pay):
    state = jnp.zeros((NST, 128), F32)
    for d in range(OWN):
        pay[d, 0:NST, :] = state.astype(BF16)
        pay[d, NST : NST + TAIL, :] = asks[d]
        if d < OWN - 1:
            decay = decayed(got[d, NST : NST + TAIL, :])
            state = decay * state + got[d, 0:NST, :].astype(F32)


def head_weights(run_rows, run_lanes, h, lanes, mask, aff, forward):
    a = run_rows[:, h : h + 1]
    b = run_lanes[h : h + 1, lanes]
    gap = a - b if forward else b - a
    return (jnp.exp2(jnp.where(mask, gap, NEG)) * aff).astype(BF16)


def lane_masks():
    which = iota((BLK, 128), 1) >> 5
    return [(which == q).astype(F32).astype(BF16) for q in range(4)]


def group_out(run_rows, run_lanes, first, lanes, mask, aff, values, masks, forward):
    ws = [
        head_weights(run_rows, run_lanes, first + q, lanes, mask, aff, forward) for q in range(4)
    ]
    return dot(
        jnp.concatenate(ws, axis=1), jnp.concatenate([values * m for m in masks], axis=0)
    )


def fore_local_body(x, wr, rd, run, step, out, mid):
    run2 = run[...] * LOG2E
    run_lanes = run2.T
    masks = lane_masks()
    mask = iota((BLK, BLK), 0) >= iota((BLK, BLK), 1)
    base = spreader()
    step_pair = split_pair(step[...])
    edge = run2[BLK - 1 : BLK, :]
    for b in range(2):
        rows = slice(b * BLK, (b + 1) * BLK)
        run_rows = run2[rows, :]
        aff = dot_t(rd[rows, :], wr[rows, :])
        if b == 0:
            side = split_pair(step[rows, :] * jnp.exp2(edge - run_rows))
            wt = turned(wr[rows, :])
        else:
            side = split_pair(jnp.exp2(run_rows - edge))
        for c in range(NCH):
            e = spread_of(base, c)
            xs = x[rows, cols(c)].astype(F32)
            values = (xs * dot(step_pair[rows, :], e)).astype(BF16)
            sides = dot(side, e)
            if b == 0:
                mid[:, cols(c)] = dot(wt, (xs * sides).astype(BF16)).astype(BF16)
            else:
                carried = sides * dot(rd[rows, :], mid[:, cols(c)])
            for k in range(2):
                lanes = slice(k * 128, (k + 1) * 128)
                o = group_out(
                    run_rows, run_lanes, 8 * c + 4 * k, rows, mask, aff, values[:, lanes], masks, True
                )
                if b == 1:
                    o = o + carried[:, lanes]
                out[rows, c * CH + k * 128 : c * CH + (k + 1) * 128] = o


def back_local_body(og, wr, rd, run, out, mid):
    run2 = run[...] * LOG2E
    run_lanes = run2.T
    masks = lane_masks()
    mask = iota((BLK, BLK), 0) <= iota((BLK, BLK), 1)
    base = spreader()
    edge = run2[BLK - 1 : BLK, :]
    for b in (1, 0):
        rows = slice(b * BLK, (b + 1) * BLK)
        run_rows = run2[rows, :]
        aff = dot_t(wr[rows, :], rd[rows, :])
        if b == 1:
            side = split_pair(jnp.exp2(run_rows - edge))
            rt = turned(rd[rows, :])
        else:
            side = split_pair(jnp.exp2(edge - run_rows))
        for c in range(NCH):
            e = spread_of(base, c)
            values = og[rows, cols(c)]
            sides = dot(side, e)
            if b == 1:
                mid[:, cols(c)] = dot(rt, (values.astype(F32) * sides).astype(BF16)).astype(BF16)
            else:
                carried = sides * dot(wr[rows, :], mid[:, cols(c)])
            for k in range(2):
                lanes = slice(k * 128, (k + 1) * 128)
                o = group_out(
                    run_rows, run_lanes, 8 * c + 4 * k, rows, mask, aff, values[:, lanes], masks, False
                )
                if b == 0:
                    o = o + carried[:, lanes]
                out[rows, c * CH + k * 128 : c * CH + (k + 1) * 128] = o


def places_body(ids, depth, asks, place_col, place_row):
    idv = ids[...].astype(F32)
    dep = depth[...]
    seq = jnp.zeros((TILES, SLOTS), F32)
    for s in range(SLOTS):
        seq = seq + jnp.where(dep == s, idv[:, s : s + 1], 0.0)
    lane = iota((128, 128), 1)
    lane_f = lane.astype(F32)
    below = (iota((128, 128), 0) > lane).astype(F32).astype(BF16)
    seen = jnp.zeros((1, 128), F32)
    total = jnp.zeros((128, 128), F32)
    for b in range(ROWS // 128):
        two = [jnp.broadcast_to(seq[:, k : k + 1], (TILES, 128)) for k in (2 * b, 2 * b + 1)]
        token = jnp.concatenate(two, axis=0).astype(jnp.int32)
        owner = token >> 8
        local = (token & 255).astype(F32)
        hot = owner == lane
        hot_f = hot.astype(F32)
        rank = dot(below, hot_f.astype(BF16)) + seen
        seen = seen + jnp.sum(hot_f, axis=0, keepdims=True)
        mine = jnp.sum(jnp.where(hot, rank, 0.0), axis=1, keepdims=True)
        mine = jnp.broadcast_to(mine, (128, 128))
        place = mine + (owner * 128).astype(F32)
        place_col[b * 128 : (b + 1) * 128, :] = place
        place_row[:, b * 128 : (b + 1) * 128] = place.T[0:8, :]
        named = jnp.where(hot, local, 0.0)
        total = total + dot(turned(named), (mine == lane_f).astype(F32).astype(BF16))
    first = iota((TAIL, 128), 0) == 0
    for o in range(OWN):
        asks[o] = jnp.where(first, total[o : o + 1, :], 0.0).astype(BF16)


def features_body(local, got, rd, run, weight, scan_out, answer):
    base = spreader()
    lead = split_pair(jnp.exp(run[...]))
    feat = jnp.zeros((TOK, FEAT), F32)
    for c in range(NCH):
        state = jnp.concatenate([got[2 * c, 0:NST, :], got[2 * c + 1, 0:NST, :]], axis=1)
        rows = local[:, cols(c)] + dot(lead, spread_of(base, c)) * dot(rd[...], state)
        rows = rows.astype(BF16)
        scan_out[:, cols(c)] = rows
        feat = feat + dot(rows, weight[cols(c), :])
    feat = feat.astype(BF16)
    asked = jnp.concatenate(
        [got[d, NST : NST + TAIL, :].astype(F32)[0:1, :] for d in range(OWN)]
        + [jnp.zeros((128 - OWN, 128), F32)],
        axis=0,
    ).T
    token = iota((128, TOK), 1).astype(F32)
    for d in range(OWN):
        pick = (asked[:, d : d + 1] == token).astype(F32).astype(BF16)
        answer[d] = dot(pick, feat).astype(BF16)


def composite_body(
    ans, place_col, place_row, depth, count, camera, gain, target, out, slots, keep, trans, grads
):
    lane_f = iota((256, 128), 1).astype(F32)
    for b in range(ROWS // 256):
        rows = slice(b * 256, (b + 1) * 256)
        place = place_col[rows, :]
        hot = jnp.concatenate(
            [(place == lane_f + 128.0 * o).astype(F32).astype(BF16) for o in range(OWN)], axis=1
        )
        slots[rows, :] = dot(hot, ans[...])
    lane = iota((TILES, 128), 1)
    left = lane < GAUSS_LANES
    dep = depth[...]
    cnt = count[...]
    cam = camera[...]
    vg = gain[...]
    wide = iota((8, FEAT), 1)
    gains = jnp.where(wide < 64, vg[:, 0:1], jnp.where(wide < 128, vg[:, 1:2], vg[:, 2:3]))
    tile_gain = jnp.zeros((TILES, FEAT), F32)
    for v in range(8):
        tile_gain = tile_gain + jnp.where(cam == v, gains[v : v + 1, :], 0.0)
    gain_a, gain_b = tile_gain[:, 0:128], tile_gain[:, 128:256]
    target_a = target[:, 0:128]
    target_b = jnp.concatenate([target[:, 128:192], jnp.zeros((TILES, 64), F32)], axis=1)
    t = jnp.ones((TILES, 128), F32)
    ra = jnp.zeros((TILES, 128), F32)
    rb = jnp.zeros((TILES, 128), F32)
    for k in range(SLOTS):
        rows = slice(k * TILES, (k + 1) * TILES)
        sa = jax.nn.sigmoid(slots[rows, 0:128])
        sb = jax.nn.sigmoid(slots[rows, 128:256])
        so = jnp.where(left, pltpu.roll(sb, 64, 1), sb)
        live = jnp.where(dep[:, k : k + 1] < cnt, 0.95, 0.0)
        a = so * live
        w = t * a
        ra = ra + w * sa
        rb = rb + w * sb
        slots[rows, 0:128] = sa
        slots[rows, 128:256] = sb
        keep[rows, :] = so
        trans[rows, :] = t
        t = t * (1.0 - a)
    ea = ra * gain_a - target_a
    eb = rb * gain_b - target_b
    ga = ea * lax.rsqrt(ea * ea + 0.01) * gain_a
    gb = jnp.where(left, eb * lax.rsqrt(eb * eb + 0.01) * gain_b, 0.0)
    dt = jnp.zeros((TILES, 128), F32)
    for k in reversed(range(SLOTS)):
        rows = slice(k * TILES, (k + 1) * TILES)
        sa = slots[rows, 0:128]
        sb = slots[rows, 128:256]
        so = keep[rows, :]
        t = trans[rows, :]
        live = jnp.where(dep[:, k : k + 1] < cnt, 0.95, 0.0)
        a = so * live
        ua = ga * sa
        ub = gb * sb
        q = ua + ub
        q = q + pltpu.roll(q, 64, 1)
        da = t * (q - dt)
        dt = a * q + (1.0 - a) * dt
        w = t * a
        grads[rows, 0:128] = (w * ua * (1.0 - sa)).astype(BF16)
        grads[rows, 128:256] = jnp.where(
            left, w * ub * (1.0 - sb), da * a * (1.0 - so)
        ).astype(BF16)
    sub_f = iota((256, ROWS), 0).astype(F32)
    place = place_row[0:1, :]
    for b in range(OWN * 128 // 256):
        hot = (place == sub_f + 256.0 * b).astype(F32).astype(BF16)
        out[b * 256 : (b + 1) * 256, :] = dot(hot, grads[...]).astype(BF16)


GAUSS_LANES = 64


def token_grad_body(homed, asked, weight, scan_out, rd, run, out_grad, pay):
    token = iota((TOK, 128), 0).astype(F32)
    hot = jnp.concatenate(
        [
            (asked[d].astype(F32)[0:1, :] == token).astype(F32).astype(BF16)
            for d in range(OWN)
        ],
        axis=1,
    )
    feat = dot(hot, homed[...])
    low = feat.astype(BF16)
    low_t = turned(low)
    base = spreader()
    lead = split_pair(jnp.exp(run[...]))
    rt = turned(rd[...])
    for c in range(NCH):
        og = dot_t(low, weight[cols(c), :]).astype(BF16)
        out_grad[:, cols(c)] = og
        scaled = (og.astype(F32) * dot(lead, spread_of(base, c))).astype(BF16)
        end = dot(rt, scaled).astype(BF16)
        part = dot(low_t, scan_out[:, cols(c)]).astype(BF16)
        for k in range(2):
            lanes = slice(k * 128, (k + 1) * 128)
            pay[2 * c + k, 0:NST, :] = end[:, lanes]
            pay[2 * c + k, NST : NST + FEAT, :] = part[:, lanes]


def scene_sum_body(got, out):
    total = jnp.zeros((FEAT, 128), F32)
    for d in range(OWN):
        total = total + got[d, NST : NST + FEAT, :].astype(F32)
    total = total.astype(BF16)
    for i in range(8):
        out[i] = total


def suffix_body(got, tails, pay):
    state = jnp.zeros((NST, 128), F32)
    for d in reversed(range(OWN)):
        pay[d, 0:NST, :] = state.astype(BF16)
        if d > 0:
            state = decayed(tails[d]) * state + got[d, 0:NST, :].astype(F32)


def all_scenes_body(scale, parts, pay_in, pay):
    del pay_in
    total = parts[0].astype(F32)
    for i in range(1, 8):
        total = total + parts[i].astype(F32)
    total = (total * scale).T
    half = total[:, 0:128].astype(BF16)
    other = total[:, 128:256].astype(BF16)
    first = pl.program_id(0) == 0
    block = jnp.where(first, half.astype(F32), other.astype(F32)).astype(BF16)
    for d in range(OWN):
        pay[d] = block


def input_grad_body(within, got, wr, run, step, grad, wgrad):
    base = spreader()
    run_v = run[...]
    tail = split_pair(jnp.exp(run_v[TOK - 1 : TOK, :] - run_v))
    steps = split_pair(step[...])
    for c in range(NCH):
        e = spread_of(base, c)
        state = jnp.concatenate([got[2 * c, 0:NST, :], got[2 * c + 1, 0:NST, :]], axis=1)
        rows = within[:, cols(c)] + dot(tail, e) * dot(wr[...], state)
        grad[:, cols(c)] = (rows * dot(steps, e)).astype(BF16)
    for d in range(OWN):
        wgrad[d * 128 : (d + 1) * 128, 0:128] = got[d, NST : NST + 128, :].astype(F32)
        wgrad[d * 128 : (d + 1) * 128, 128:256] = got[d, NST + 128 : NST + 256, :].astype(F32)


def swap(x, axes):
    return lax.all_to_all(x, axes, split_axis=0, concat_axis=0, tiled=True)


def shards(
    ssm_input,
    write_basis,
    read_basis,
    step_size,
    log_decay,
    head_weight,
    block_list,
    block_count,
    depth_order,
    camera_index,
    view_gain,
    target_color,
):
    x, wr, rd = ssm_input[0], write_basis[0], read_basis[0]
    depth = depth_order[0]
    tail_spec = pl.BlockSpec((OWN, TAIL, 128), lambda *_: (0, NST // TAIL, 0))
    vmem = pl.BlockSpec(memory_space=pltpu.VMEM)

    pay, run, step = call(
        local_end_body,
        [((OWN, NST + TAIL, 128), BF16), ((TOK, 128), F32), ((TOK, 128), F32)],
        flops=1 << 29,
    )(x, wr, step_size[0], log_decay[0])
    ends = swap(pay, SEQ)
    asks, place_col, place_row = call(
        places_body,
        [((OWN, TAIL, 128), BF16), ((ROWS, 128), F32), ((8, ROWS), F32)],
        flops=1 << 31,
    )(block_list[0], depth)
    (local,) = call(
        fore_local_body,
        [((TOK, WID), F32)],
        scratch=[pltpu.VMEM((NST, WID), BF16)],
        flops=1 << 32,
    )(x, wr, rd, run, step)
    (pay,) = call(prefix_body, [((OWN, NST + TAIL, 128), BF16)])(ends, asks)
    states = swap(pay, SEQ)
    scan_out, answer = call(
        features_body, [((TOK, WID), BF16), ((OWN, 128, FEAT), BF16)], flops=1 << 31
    )(local, states, rd, run, head_weight)
    answered = swap(answer, SEQ)
    (outgoing,) = call(
        composite_body,
        [((OWN * 128, FEAT), BF16)],
        scratch=[
            pltpu.VMEM((ROWS, FEAT), F32),
            pltpu.VMEM((ROWS, 128), F32),
            pltpu.VMEM((ROWS, 128), F32),
            pltpu.VMEM((ROWS, FEAT), BF16),
        ],
        flops=1 << 32,
    )(
        answered.reshape(OWN * 128, FEAT),
        place_col,
        place_row,
        depth,
        block_count[0][:, None],
        camera_index[0][:, None],
        view_gain[0],
        target_color[0],
    )
    homed = swap(outgoing.reshape(OWN, 128, FEAT), SEQ)
    out_grad, pay = call(
        token_grad_body,
        [((TOK, WID), BF16), ((OWN, NST + FEAT, 128), BF16)],
        in_specs=[vmem, tail_spec, vmem, vmem, vmem, vmem],
        out_specs=[vmem, vmem],
        grid=(1,),
        flops=1 << 31,
    )(homed.reshape(OWN * 128, FEAT), states, head_weight, scan_out, rd, run)
    back = swap(pay, SEQ)
    (within,) = call(
        back_local_body,
        [((TOK, WID), F32)],
        scratch=[pltpu.VMEM((NST, WID), BF16)],
        flops=1 << 32,
    )(out_grad, wr, rd, run)
    (scene_part,) = call(scene_sum_body, [((8, FEAT, 128), BF16)])(back)
    scene_parts = swap(scene_part, ("dp",))
    (pay,) = call(
        suffix_body,
        [((OWN, NST + FEAT, 128), BF16)],
        in_specs=[pl.BlockSpec((OWN, NST, 128), lambda *_: (0, 0, 0)), tail_spec],
        out_specs=[pl.BlockSpec((OWN, NST, 128), lambda *_: (0, 0, 0))],
        grid=(1,),
    )(back, ends)
    scale = 1.0 / np.sqrt(np.float64(lax.axis_size("dp") * TOK * lax.axis_size(SEQ)))
    (pay,) = call(
        lambda *refs: all_scenes_body(np.float32(scale), *refs),
        [((OWN, NST + FEAT, 128), BF16)],
        in_specs=[vmem, pl.BlockSpec(memory_space=pl.ANY)],
        out_specs=[pl.BlockSpec((OWN, 128, 128), lambda i: (0, 1 + i, 0))],
        grid=(2,),
        alias={1: 0},
    )(scene_parts, pay)
    states_back = swap(pay, SEQ)
    grad, wgrad = call(
        input_grad_body, [((TOK, WID), BF16), ((WID, FEAT), F32)], flops=1 << 30
    )(within, states_back, wr, run, step)
    return grad[None], wgrad


def solution(mesh):
    torus = Mesh(mesh.devices.reshape(mesh.shape["dp"], 4, 4), ("dp", "seq_0", "seq_1"))
    in_specs = (
        P("dp", SEQ, None),
        P("dp", SEQ, None),
        P("dp", SEQ, None),
        P("dp", SEQ, None),
        P("dp", SEQ, None),
        P(),
        P("dp", SEQ, None),
        P("dp", SEQ),
        P("dp", SEQ, None),
        P("dp", SEQ),
        P("dp", None, None),
        P("dp", SEQ, None),
    )
    out_specs = (P("dp", SEQ, None), P())
    return jax.shard_map(
        shards, mesh=torus, in_specs=in_specs, out_specs=out_specs, check_vma=False
    )
```

profile of v0, /device:TPU:0, one launch (start us, length us, event | category | flops | bytes accessed | tf_op | source)
XLA Modules:
  0.0 164.8 jit_solution(15473128373810449279)
XLA Ops:
  1.6 0.9 copy.16
  3.4 1.2 copy-done.4
  4.6 1.8 %shard_map.131 = (bf16[16,144,128]{2,1,0:T(8,128)(2,1)}, f32[256,128]{1,0:T(8,128)S(1)}, f32[256,128]{1,0:T(8,128)S(1)}) custom-call(bf16[256,2048]{1,0:T(8,128)(2,1)S(1)} %bitcast.28, bf16[256,128]{1,0:T(8,128)(2,1)S(1)} %bitcast.20, f32[256,64]{1,0:T(8,128)S(1)} %bitcast.18, f32[256,64]{1,0:T(8,128)S(1)} %bitcast.19), custom_call_target="tpu_custom_call" | custom-call | flops 536870912 | bytes 4194304 | tf_op jit(solution)/shard_map/pallas_call | solution.py:449
  6.4 8.0 %all-to-all-start = ((bf16[16,144,128]{2,1,0:T(8,128)(2,1)}), bf16[16,144,128]{2,1,0:T(8,128)(2,1)S(1)}, u32[]{:S(2)}, u32[]{:S(2)}) async-start(bf16[16,144,128]{2,1,0:T(8,128)(2,1)} %get-tuple-element.16), calls=%async_computation | async-start | bytes 1179648 | tf_op jit(solution)/shard_map/all_to_all | solution.py:427
  14.6 1.7 %shard_map.133 = (bf16[16,16,128]{2,1,0:T(8,128)(2,1)S(1)}, f32[1024,128]{1,0:T(8,128)S(1)}, f32[8,1024]{1,0:T(8,128)S(1)}) custom-call(s32[64,16]{1,0:T(8,128)S(1)} %bitcast.26, s32[64,16]{1,0:T(8,128)S(1)} %bitcast.24), custom_call_target="tpu_custom_call" | custom-call | flops 2147483648 | bytes 4194304 | tf_op jit(solution)/shard_map/pallas_call | solution.py:455
  16.3 9.9 %all-to-all-done.got.tails = bf16[16,144,128]{2,1,0:T(8,128)(2,1)S(1)} async-done(((bf16[16,144,128]{2,1,0:T(8,128)(2,1)}), bf16[16,144,128]{2,1,0:T(8,128)(2,1)S(1)}, u32[]{:S(2)}, u32[]{:S(2)}) %all-to-all-start) | async-done | bytes 589856 | tf_op jit(solution)/shard_map/all_to_all | solution.py:427
  26.3 1.0 shard_map.134
  27.2 3.8 %all-to-all-start.1 = ((bf16[16,144,128]{2,1,0:T(8,128)(2,1)}), bf16[16,144,128]{2,1,0:T(8,128)(2,1)S(1)}, u32[]{:S(2)}, u32[]{:S(2)}) async-start(bf16[16,144,128]{2,1,0:T(8,128)(2,1)} %shard_map.134), calls=%async_computation.1 | async-start | bytes 1179648 | tf_op jit(solution)/shard_map/all_to_all | solution.py:427
  31.1 4.3 %shard_map.132.local = f32[256,2048]{1,0:T(8,128)S(1)} custom-call(bf16[256,2048]{1,0:T(8,128)(2,1)S(1)} %bitcast.29, bf16[256,128]{1,0:T(8,128)(2,1)S(1)} %bitcast.21, bf16[256,128]{1,0:T(8,128)(2,1)S(1)} %bitcast.31, f32[256,128]{1,0:T(8,128)S(1)} %get-tuple-element.14.run, f32[256,128]{1,0:T(8,128)S(1)} %get-tuple-element.15.step), custom_call_target="tpu_custom_call" | custom-call | flops 4294967296 | bytes 4194304 | tf_op jit(solution)/shard_map/pallas_call | solution.py:460
  35.3 1.3 copy-done.10
  36.7 5.4 %all-to-all-done.1.got.asked = bf16[16,144,128]{2,1,0:T(8,128)(2,1)S(1)} async-done(((bf16[16,144,128]{2,1,0:T(8,128)(2,1)}), bf16[16,144,128]{2,1,0:T(8,128)(2,1)S(1)}, u32[]{:S(2)}, u32[]{:S(2)}) %all-to-all-start.1) | async-done | bytes 589856 | tf_op jit(solution)/shard_map/all_to_all | solution.py:427
  42.1 1.2 copy-done.6
  43.3 1.6 copy-done.11
  44.9 2.8 %shard_map.135 = (bf16[256,2048]{1,0:T(8,128)(2,1)S(1)}, bf16[16,128,256]{2,1,0:T(8,128)(2,1)}) custom-call(f32[256,2048]{1,0:T(8,128)S(1)} %copy-done.11, bf16[16,144,128]{2,1,0:T(8,128)(2,1)S(1)} %all-to-all-done.1.got.asked, bf16[256,128]{1,0:T(8,128)(2,1)S(1)} %bitcast.32, f32[256,128]{1,0:T(8,128)S(1)} %get-tuple-element.14.run, ...), custom_call_target="tpu_custom_call" | custom-call | flops 2147483648 | bytes 4194304 | tf_op jit(solution)/shard_map/pallas_call | solution.py:468
  47.7 1.0 copy-done.12
  48.7 3.8 %all-to-all-start.2 = ((bf16[16,128,256]{2,1,0:T(8,128)(2,1)}), bf16[16,128,256]{2,1,0:T(8,128)(2,1)S(1)}, u32[]{:S(2)}, u32[]{:S(2)}) async-start(bf16[16,128,256]{2,1,0:T(8,128)(2,1)} %get-tuple-element.18), calls=%async_computation.2 | async-start | bytes 2097152 | tf_op jit(solution)/shard_map/all_to_all | solution.py:427
  52.8 14.4 %all-to-all-done.2 = bf16[16,128,256]{2,1,0:T(8,128)(2,1)S(1)} async-done(((bf16[16,128,256]{2,1,0:T(8,128)(2,1)}), bf16[16,128,256]{2,1,0:T(8,128)(2,1)S(1)}, u32[]{:S(2)}, u32[]{:S(2)}) %all-to-all-start.2) | async-done | bytes 1048608 | tf_op jit(solution)/shard_map/all_to_all | solution.py:427
  67.1 1.0 copy-done.17
  68.2 3.1 %shard_map.136 = bf16[2048,256]{1,0:T(8,128)(2,1)S(1)} custom-call(bf16[2048,256]{1,0:T(8,128)(2,1)S(1)} %bitcast.15, f32[1024,128]{1,0:T(8,128)S(1)} %copy-done.17, f32[8,1024]{1,0:T(8,128)S(1)} %get-tuple-element.20.place_row, s32[64,16]{1,0:T(8,128)S(1)} %bitcast.25, s32[64,1]{1,0:T(8,128)S(1)} %copy.19.count, s32[64,1]{1,0:T(8,128)S(1)} %copy.20.camera, ...), custom_call_target="tpu_custom_call" | custom-call | flops 4294967296 | bytes 4194304 | tf_op jit(solution)/shard_map/pallas_call | solution.py:472
  71.3 18.7 %all_to_all.35 = bf16[16,128,256]{2,1,0:T(8,128)(2,1)S(1)} all-to-all(bf16[16,128,256]{2,1,0:T(8,128)(2,1)S(1)} %bitcast.16), channel_id=1, replica_groups=mesh['dp'=8,'seq_0'=4,'seq_1'=4] {'seq_0','seq_1'}, dimensions={0} | all-to-all | bytes 2097152 | tf_op jit(solution)/shard_map/all_to_all | solution.py:427
  90.1 2.9 %shard_map.137 = (bf16[256,2048]{1,0:T(8,128)(2,1)S(1)}, bf16[16,384,128]{2,1,0:T(8,128)(2,1)S(1)}) custom-call(bf16[2048,256]{1,0:T(8,128)(2,1)S(1)} %bitcast.17, bf16[16,144,128]{2,1,0:T(8,128)(2,1)S(1)} %all-to-all-done.1.got.asked, bf16[2048,256]{1,0:T(8,128)(2,1)S(1)} %copy-done.7, bf16[256,2048]{1,0:T(8,128)(2,1)S(1)} %copy-done.13, ...), custom_call_target="tpu_custom_call" | custom-call | flops 2147483648 | bytes 4194304 | tf_op jit(solution)/shard_map/pallas_call | solution.py:493
  93.0 22.9 %all_to_all.36.got = bf16[16,384,128]{2,1,0:T(8,128)(2,1)S(1)} all-to-all(bf16[16,384,128]{2,1,0:T(8,128)(2,1)S(1)} %get-tuple-element.23), channel_id=1, replica_groups=mesh['dp'=8,'seq_0'=4,'seq_1'=4] {'seq_0','seq_1'}, dimensions={0} | all-to-all | bytes 3145728 | tf_op jit(solution)/shard_map/all_to_all | solution.py:427
  116.9 4.5 %all-to-all-start.5 = ((bf16[8,256,128]{2,1,0:T(8,128)(2,1)}), bf16[8,256,128]{2,1,0:T(8,128)(2,1)S(1)}, u32[]{:S(2)}, u32[]{:S(2)}) async-start(bf16[8,256,128]{2,1,0:T(8,128)(2,1)} %shard_map.139), calls=%async_computation.5 | async-start | bytes 1048576 | tf_op jit(solution)/shard_map/all_to_all | solution.py:427
  121.3 1.0 shard_map.140.refs_1_
  122.3 9.4 %all-to-all-done.5.refs_0_ = bf16[8,256,128]{2,1,0:T(8,128)(2,1)S(1)} async-done(((bf16[8,256,128]{2,1,0:T(8,128)(2,1)}), bf16[8,256,128]{2,1,0:T(8,128)(2,1)S(1)}, u32[]{:S(2)}, u32[]{:S(2)}) %all-to-all-start.5) | async-done | bytes 524320 | tf_op jit(solution)/shard_map/all_to_all | solution.py:427
  131.7 1.2 shard_map.141
  132.8 3.8 %all-to-all-start.6 = ((bf16[16,384,128]{2,1,0:T(8,128)(2,1)}), bf16[16,384,128]{2,1,0:T(8,128)(2,1)S(1)}, u32[]{:S(2)}, u32[]{:S(2)}) async-start(bf16[16,384,128]{2,1,0:T(8,128)(2,1)} %shard_map.141), calls=%async_computation.6 | async-start | bytes 3145728 | tf_op jit(solution)/shard_map/all_to_all | solution.py:427
  136.7 3.1 %shard_map.138.within = f32[256,2048]{1,0:T(8,128)S(1)} custom-call(bf16[256,2048]{1,0:T(8,128)(2,1)S(1)} %copy-done.15, bf16[256,128]{1,0:T(8,128)(2,1)S(1)} %bitcast.22, bf16[256,128]{1,0:T(8,128)(2,1)S(1)} %bitcast.34, f32[256,128]{1,0:T(8,128)S(1)} %get-tuple-element.14.run), custom_call_target="tpu_custom_call" | custom-call | flops 4294967296 | bytes 4194304 | tf_op jit(solution)/shard_map/pallas_call | solution.py:502
  139.8 1.3 copy-done
  141.2 19.4 %all-to-all-done.6.got = bf16[16,384,128]{2,1,0:T(8,128)(2,1)S(1)} async-done(((bf16[16,384,128]{2,1,0:T(8,128)(2,1)}), bf16[16,384,128]{2,1,0:T(8,128)(2,1)S(1)}, u32[]{:S(2)}, u32[]{:S(2)}) %all-to-all-start.6) | async-done | bytes 1572896 | tf_op jit(solution)/shard_map/all_to_all | solution.py:427
  160.5 1.6 copy-done.1
  162.1 2.7 %shard_map.142 = (bf16[256,2048]{1,0:T(8,128)(2,1)}, f32[2048,256]{1,0:T(8,128)}) custom-call(f32[256,2048]{1,0:T(8,128)S(1)} %copy-done.1, bf16[16,384,128]{2,1,0:T(8,128)(2,1)S(1)} %all-to-all-done.6.got, bf16[256,128]{1,0:T(8,128)(2,1)S(1)} %bitcast.23, f32[256,128]{1,0:T(8,128)S(1)} %get-tuple-element.14.run, f32[256,128]{1,0:T(8,128)S(1)} %get-tuple-element.15.step), custom_call_target="tpu_custom_call" | custom-call | flops 1073741824 | bytes 4194304 | tf_op jit(solution)/shard_map/pallas_call | solution.py:527
  (45 shorter events, 3.2 us)
Async XLA Ops:
  2.5 0.8 copy-start.2
  3.3 1.2 copy-start.4
  4.6 9.8 %copy-start.18 = (s32[1,64,16]{1,2,0:T(8,128)S(1)}, s32[1,64,16]{1,2,0:T(8,128)}, u32[]{:S(2)}) copy-start(s32[1,64,16]{1,2,0:T(8,128)} %param.18) | copy-start | bytes 12292
  4.6 9.9 %copy-start.19 = (s32[1,64,16]{1,2,0:T(8,128)S(1)}, s32[1,64,16]{1,2,0:T(8,128)}, u32[]{:S(2)}) copy-start(s32[1,64,16]{1,2,0:T(8,128)} %param.20) | copy-start | bytes 12292
  6.4 19.9 %all-to-all-start = ((bf16[16,144,128]{2,1,0:T(8,128)(2,1)}), bf16[16,144,128]{2,1,0:T(8,128)(2,1)S(1)}, u32[]{:S(2)}, u32[]{:S(2)}) async-start(bf16[16,144,128]{2,1,0:T(8,128)(2,1)} %get-tuple-element.16), calls=%async_computation | async-start | bytes 1179648 | tf_op jit(solution)/shard_map/all_to_all | solution.py:427
  16.3 10.9 %copy-start.16 = (f32[1024,128]{1,0:T(8,128)}, f32[1024,128]{1,0:T(8,128)S(1)}, u32[]{:S(2)}) copy-start(f32[1024,128]{1,0:T(8,128)S(1)} %get-tuple-element.19.place_col) | copy-start | bytes 1572868
  16.3 14.7 %copy-start.3 = (bf16[1,256,128]{2,1,0:T(8,128)(2,1)S(1)}, bf16[1,256,128]{2,1,0:T(8,128)(2,1)}, u32[]{:S(2)}) copy-start(bf16[1,256,128]{2,1,0:T(8,128)(2,1)} %param.13) | copy-start | bytes 196612
  16.3 14.7 %copy-start.5 = (bf16[1,256,2048]{2,1,0:T(8,128)(2,1)S(1)}, bf16[1,256,2048]{2,1,0:T(8,128)(2,1)}, u32[]{:S(2)}) copy-start(bf16[1,256,2048]{2,1,0:T(8,128)(2,1)} %param.12) | copy-start | bytes 3145732
  16.3 14.7 %copy-start.9 = (bf16[1,256,128]{2,1,0:T(8,128)(2,1)S(1)}, bf16[1,256,128]{2,1,0:T(8,128)(2,1)}, u32[]{:S(2)}) copy-start(bf16[1,256,128]{2,1,0:T(8,128)(2,1)} %param.14) | copy-start | bytes 196612
  27.2 14.8 %all-to-all-start.1 = ((bf16[16,144,128]{2,1,0:T(8,128)(2,1)}), bf16[16,144,128]{2,1,0:T(8,128)(2,1)S(1)}, u32[]{:S(2)}, u32[]{:S(2)}) async-start(bf16[16,144,128]{2,1,0:T(8,128)(2,1)} %shard_map.134), calls=%async_computation.1 | async-start | bytes 1179648 | tf_op jit(solution)/shard_map/all_to_all | solution.py:427
  35.3 1.3 copy-start.10
  42.1 1.2 copy-start.6
  43.3 1.6 copy-start.11
  47.7 1.0 copy-start.12
  48.6 3.8 %copy-start.20 = (f32[1,8,3]{1,0,2:T(1,128)S(1)}, f32[1,8,3]{1,0,2:T(1,128)}, u32[]{:S(2)}) copy-start(f32[1,8,3]{1,0,2:T(1,128)} %param.22) | copy-start | bytes 292
  48.6 3.9 %copy-start.21 = (s32[1,64]{1,0:T(1,128)S(1)}, s32[1,64]{1,0:T(1,128)}, u32[]{:S(2)}) copy-start(s32[1,64]{1,0:T(1,128)} %param.19) | copy-start | bytes 772
  48.7 4.0 %copy-start.22 = (s32[1,64]{1,0:T(1,128)S(1)}, s32[1,64]{1,0:T(1,128)}, u32[]{:S(2)}) copy-start(s32[1,64]{1,0:T(1,128)} %param.21) | copy-start | bytes 772
  48.7 18.5 %copy-start.8 = (f32[1,64,192]{2,1,0:T(8,128)S(1)}, f32[1,64,192]{2,1,0:T(8,128)}, u32[]{:S(2)}) copy-start(f32[1,64,192]{2,1,0:T(8,128)} %param.23) | copy-start | bytes 147460
  48.7 18.5 %all-to-all-start.2 = ((bf16[16,128,256]{2,1,0:T(8,128)(2,1)}), bf16[16,128,256]{2,1,0:T(8,128)(2,1)S(1)}, u32[]{:S(2)}, u32[]{:S(2)}) async-start(bf16[16,128,256]{2,1,0:T(8,128)(2,1)} %get-tuple-element.18), calls=%async_computation.2 | async-start | bytes 2097152 | tf_op jit(solution)/shard_map/all_to_all | solution.py:427
  67.1 1.0 copy-start.17
  71.3 18.7 %copy-start.7 = (bf16[2048,256]{1,0:T(8,128)(2,1)S(1)}, bf16[2048,256]{1,0:T(8,128)(2,1)}, u32[]{:S(2)}) copy-start(bf16[2048,256]{1,0:T(8,128)(2,1)} %weight.3) | copy-start | bytes 3145732
  71.3 18.7 %copy-start.13 = (bf16[256,2048]{1,0:T(8,128)(2,1)S(1)}, bf16[256,2048]{1,0:T(8,128)(2,1)}, u32[]{:S(2)}) copy-start(bf16[256,2048]{1,0:T(8,128)(2,1)} %copy-done.12) | copy-start | bytes 3145732
  93.0 22.9 %copy-start.14 = (bf16[256,2048]{1,0:T(8,128)(2,1)}, bf16[256,2048]{1,0:T(8,128)(2,1)S(1)}, u32[]{:S(2)}) copy-start(bf16[256,2048]{1,0:T(8,128)(2,1)S(1)} %get-tuple-element.22.og) | copy-start | bytes 3145732
  116.9 14.8 %all-to-all-start.5 = ((bf16[8,256,128]{2,1,0:T(8,128)(2,1)}), bf16[8,256,128]{2,1,0:T(8,128)(2,1)S(1)}, u32[]{:S(2)}, u32[]{:S(2)}) async-start(bf16[8,256,128]{2,1,0:T(8,128)(2,1)} %shard_map.139), calls=%async_computation.5 | async-start | bytes 1048576 | tf_op jit(solution)/shard_map/all_to_all | solution.py:427
  132.8 3.9 %copy-start.15 = (bf16[256,2048]{1,0:T(8,128)(2,1)S(1)}, bf16[256,2048]{1,0:T(8,128)(2,1)}, u32[]{:S(2)}) copy-start(bf16[256,2048]{1,0:T(8,128)(2,1)} %copy-done.14) | copy-start | bytes 3145732
  132.8 27.7 %all-to-all-start.6 = ((bf16[16,384,128]{2,1,0:T(8,128)(2,1)}), bf16[16,384,128]{2,1,0:T(8,128)(2,1)S(1)}, u32[]{:S(2)}, u32[]{:S(2)}) async-start(bf16[16,384,128]{2,1,0:T(8,128)(2,1)} %shard_map.141), calls=%async_computation.6 | async-start | bytes 3145728 | tf_op jit(solution)/shard_map/all_to_all | solution.py:427
  139.8 1.3 copy-start
  160.5 1.6 copy-start.1
where the time goes:
time: 166 us; the launch traced here: 165 us
  waiting for transfers between devices  58.5 us (35%)
  blocking collectives  41.6 us (25%)
  Pallas kernels  26.5 us (16%)
  starting transfers between devices  23.9 us (14%)
  local copies, waits for them, and re-layouts  13.5 us (8%)
    all_to_all x5, waiting for transfers between devices, swap(): return lax.all_to_all(x, axes, split_axis=0, concat_axis=0, tiled=True)  58.5 us
    all_to_all x2, blocking collectives, swap(): return lax.all_to_all(x, axes, split_axis=0, concat_axis=0, tiled=True)  41.6 us
    all_to_all x5, starting transfers between devices, swap(): return lax.all_to_all(x, axes, split_axis=0, concat_axis=0, tiled=True)  23.9 us
    unnamed x50, local copies, waits for them, and re-layouts  13.2 us
    pallas_call x1, Pallas kernels, shards(): call(fore_local_body, [((TOK, WID), F32)], scratch=[pltpu.VMEM((NST, WID)...  4.26 us
  transfers between devices with their start and end apart: 5, of which 5 were waited for; matrix products, arithmetic and copies ran while one was open for 0% of the time, Pallas kernels for 6%

commit v1 on v0

--- a/solution.py
+++ b/solution.py
@@ -61,28 +61,52 @@
     return slice(c * CH, (c + 1) * CH)
 
 
-def call(body, outs, scratch=(), in_specs=None, out_specs=None, limit=32, flops=0, grid=None, alias=None):
-    kwargs = {}
-    if in_specs is not None:
-        kwargs["in_specs"] = in_specs
-    if out_specs is not None:
-        kwargs["out_specs"] = out_specs
-    if grid is not None:
-        kwargs["grid"] = grid
+ANY = pl.BlockSpec(memory_space=pl.ANY)
+VMEM = pl.BlockSpec(memory_space=pltpu.VMEM)
+TAIL_SPEC = pl.BlockSpec((OWN, TAIL, 128), lambda *_: (0, NST // TAIL, 0))
+
+
+def near(shape, dtype):
+    return pltpu.VMEM(shape, dtype)
+
+
+def held(x):
+    return pltpu.with_memory_space_constraint(x, pltpu.VMEM)
+
+
+def far(x):
+    return pltpu.with_memory_space_constraint(x, pltpu.HBM)
+
+
+def call(body, outs, ins, out_specs, scratch=(), limit=16, flops=0, grid=()):
     return pl.pallas_call(
         body,
-        out_shape=[jax.ShapeDtypeStruct(s, d) for s, d in outs],
-        scratch_shapes=list(scratch),
+        out_shape=[
+            (near if len(o) == 3 else jax.ShapeDtypeStruct)(o[0], o[1]) for o in outs
+        ],
+        grid_spec=pl.GridSpec(
+            grid=grid, in_specs=ins, out_specs=out_specs, scratch_shapes=list(scratch)
+        ),
         compiler_params=pltpu.CompilerParams(vmem_limit_bytes=limit << 20),
         cost_estimate=pl.CostEstimate(flops=flops, transcendentals=0, bytes_accessed=4 << 20),
-        input_output_aliases=alias or {},
-        **kwargs,
-    )
-
-
-def local_end_body(x, wr, step, logd, pay, run_out, step_out):
-    ld = jnp.concatenate([logd[...], logd[...]], axis=1)
-    st = jnp.concatenate([step[...], step[...]], axis=1)
+    )
+
+
+def local_end_body(
+    x_far, wr_far, step_far, logd_far, pay, run_out, step_out, x, wr, step, logd, sem
+):
+    moves = [
+        pltpu.make_async_copy(a, b, sem.at[k])
+        for k, (a, b) in enumerate(
+            ((logd_far, logd), (step_far, step), (wr_far, wr), (x_far, x))
+        )
+    ]
+    for m in moves:
+        m.start()
+    moves[0].wait()
+    moves[1].wait()
+    ld = jnp.concatenate([logd[...], logd[...]], axis=0).T
+    st = jnp.concatenate([step[...], step[...]], axis=0).T
     row = iota((TOK, 2 * HEADS), 0)
     run = ld
     s = 1
@@ -99,8 +123,10 @@
     trow = iota((TAIL, 2 * HEADS), 0)
     tails = jnp.where(trow == 0, t1, jnp.where(trow == 1, t2, jnp.where(trow == 2, t3, 0.0)))
     tails = jnp.where(iota((TAIL, 2 * HEADS), 1) < HEADS, tails, 0.0).astype(BF16)
+    moves[2].wait()
     wt = turned(wr[...])
     base = spreader()
+    moves[3].wait()
     for c in range(NCH):
         e = spread_of(base, c)
         xs = (x[:, cols(c)].astype(F32) * dot(pair, e)).astype(BF16)
@@ -219,12 +245,22 @@
                 out[rows, c * CH + k * 128 : c * CH + (k + 1) * 128] = o
 
 
-def places_body(ids, depth, asks, place_col, place_row):
+def places_body(ids, depth, count, camera, gain, asks, place_col, place_row, live, tile_gain):
     idv = ids[...].astype(F32)
     dep = depth[...]
-    seq = jnp.zeros((TILES, SLOTS), F32)
+    seq = jnp.zeros((SLOTS, TILES), F32)
     for s in range(SLOTS):
-        seq = seq + jnp.where(dep == s, idv[:, s : s + 1], 0.0)
+        seq = seq + jnp.where(dep == s, idv[s : s + 1, :], 0.0)
+    seq = seq.T
+    live[...] = jnp.where(dep < count[...], 0.95, 0.0).T
+    hot = (iota((8, TILES), 0) == camera[...]).astype(F32).T
+    vg = gain[...].T
+    wide = iota((8, FEAT), 1)
+    gains = jnp.where(wide < 64, vg[:, 0:1], jnp.where(wide < 128, vg[:, 1:2], vg[:, 2:3]))
+    per_tile = jnp.zeros((TILES, FEAT), F32)
+    for v in range(8):
+        per_tile = per_tile + hot[:, v : v + 1] * gains[v : v + 1, :]
+    tile_gain[...] = per_tile
     lane = iota((128, 128), 1)
     lane_f = lane.astype(F32)
     below = (iota((128, 128), 0) > lane).astype(F32).astype(BF16)
@@ -254,6 +290,11 @@
 def features_body(local, got, rd, run, weight, scan_out, answer):
     base = spreader()
     lead = split_pair(jnp.exp(run[...]))
+    asked = jnp.concatenate(
+        [got[d, NST : NST + TAIL, :].astype(F32)[0:1, :] for d in range(OWN)]
+        + [jnp.zeros((128 - OWN, 128), F32)],
+        axis=0,
+    ).T
     feat = jnp.zeros((TOK, FEAT), F32)
     for c in range(NCH):
         state = jnp.concatenate([got[2 * c, 0:NST, :], got[2 * c + 1, 0:NST, :]], axis=1)
@@ -262,11 +303,6 @@
         scan_out[:, cols(c)] = rows
         feat = feat + dot(rows, weight[cols(c), :])
     feat = feat.astype(BF16)
-    asked = jnp.concatenate(
-        [got[d, NST : NST + TAIL, :].astype(F32)[0:1, :] for d in range(OWN)]
-        + [jnp.zeros((128 - OWN, 128), F32)],
-        axis=0,
-    ).T
     token = iota((128, TOK), 1).astype(F32)
     for d in range(OWN):
         pick = (asked[:, d : d + 1] == token).astype(F32).astype(BF16)
@@ -274,7 +310,7 @@
 
 
 def composite_body(
-    ans, place_col, place_row, depth, count, camera, gain, target, out, slots, keep, trans, grads
+    ans, place_col, place_row, live, tile_gain, target, out, slots, keep, trans, grads
 ):
     lane_f = iota((256, 128), 1).astype(F32)
     for b in range(ROWS // 256):
@@ -286,15 +322,6 @@
         slots[rows, :] = dot(hot, ans[...])
     lane = iota((TILES, 128), 1)
     left = lane < GAUSS_LANES
-    dep = depth[...]
-    cnt = count[...]
-    cam = camera[...]
-    vg = gain[...]
-    wide = iota((8, FEAT), 1)
-    gains = jnp.where(wide < 64, vg[:, 0:1], jnp.where(wide < 128, vg[:, 1:2], vg[:, 2:3]))
-    tile_gain = jnp.zeros((TILES, FEAT), F32)
-    for v in range(8):
-        tile_gain = tile_gain + jnp.where(cam == v, gains[v : v + 1, :], 0.0)
     gain_a, gain_b = tile_gain[:, 0:128], tile_gain[:, 128:256]
     target_a = target[:, 0:128]
     target_b = jnp.concatenate([target[:, 128:192], jnp.zeros((TILES, 64), F32)], axis=1)
@@ -306,8 +333,7 @@
         sa = jax.nn.sigmoid(slots[rows, 0:128])
         sb = jax.nn.sigmoid(slots[rows, 128:256])
         so = jnp.where(left, pltpu.roll(sb, 64, 1), sb)
-        live = jnp.where(dep[:, k : k + 1] < cnt, 0.95, 0.0)
-        a = so * live
+        a = so * live[:, k : k + 1]
         w = t * a
         ra = ra + w * sa
         rb = rb + w * sb
@@ -327,8 +353,7 @@
         sb = slots[rows, 128:256]
         so = keep[rows, :]
         t = trans[rows, :]
-        live = jnp.where(dep[:, k : k + 1] < cnt, 0.95, 0.0)
-        a = so * live
+        a = so * live[:, k : k + 1]
         ua = ga * sa
         ub = gb * sb
         q = ua + ub
@@ -377,50 +402,34 @@
             pay[2 * c + k, NST : NST + FEAT, :] = part[:, lanes]
 
 
-def scene_sum_body(got, out):
+def suffix_body(got, tails, pay, part):
+    state = jnp.zeros((NST, 128), F32)
+    for d in reversed(range(OWN)):
+        pay[d] = state.astype(BF16)
+        if d > 0:
+            state = decayed(tails[d]) * state + got[d, 0:NST, :].astype(F32)
     total = jnp.zeros((FEAT, 128), F32)
     for d in range(OWN):
         total = total + got[d, NST : NST + FEAT, :].astype(F32)
-    total = total.astype(BF16)
-    for i in range(8):
-        out[i] = total
-
-
-def suffix_body(got, tails, pay):
-    state = jnp.zeros((NST, 128), F32)
-    for d in reversed(range(OWN)):
-        pay[d, 0:NST, :] = state.astype(BF16)
-        if d > 0:
-            state = decayed(tails[d]) * state + got[d, 0:NST, :].astype(F32)
-
-
-def all_scenes_body(scale, parts, pay_in, pay):
-    del pay_in
-    total = parts[0].astype(F32)
-    for i in range(1, 8):
-        total = total + parts[i].astype(F32)
-    total = (total * scale).T
-    half = total[:, 0:128].astype(BF16)
-    other = total[:, 128:256].astype(BF16)
-    first = pl.program_id(0) == 0
-    block = jnp.where(first, half.astype(F32), other.astype(F32)).astype(BF16)
+    part[...] = total
+
+
+def spread_weight_body(scale, part, pay):
+    block = (part[...] * scale).T.astype(BF16)
     for d in range(OWN):
         pay[d] = block
 
 
-def input_grad_body(within, got, wr, run, step, grad, wgrad):
+def input_grad_body(within, got, wr, run, step, grad):
     base = spreader()
     run_v = run[...]
     tail = split_pair(jnp.exp(run_v[TOK - 1 : TOK, :] - run_v))
     steps = split_pair(step[...])
     for c in range(NCH):
         e = spread_of(base, c)
-        state = jnp.concatenate([got[2 * c, 0:NST, :], got[2 * c + 1, 0:NST, :]], axis=1)
+        state = jnp.concatenate([got[2 * c], got[2 * c + 1]], axis=1)
         rows = within[:, cols(c)] + dot(tail, e) * dot(wr[...], state)
         grad[:, cols(c)] = (rows * dot(steps, e)).astype(BF16)
-    for d in range(OWN):
-        wgrad[d * 128 : (d + 1) * 128, 0:128] = got[d, NST : NST + 128, :].astype(F32)
-        wgrad[d * 128 : (d + 1) * 128, 128:256] = got[d, NST + 128 : NST + 256, :].astype(F32)
 
 
 def swap(x, axes):
@@ -442,91 +451,118 @@
     target_color,
 ):
     x, wr, rd = ssm_input[0], write_basis[0], read_basis[0]
-    depth = depth_order[0]
-    tail_spec = pl.BlockSpec((OWN, TAIL, 128), lambda *_: (0, NST // TAIL, 0))
-    vmem = pl.BlockSpec(memory_space=pltpu.VMEM)
+    buf = pltpu.VMEM
 
     pay, run, step = call(
         local_end_body,
-        [((OWN, NST + TAIL, 128), BF16), ((TOK, 128), F32), ((TOK, 128), F32)],
+        [((OWN, NST + TAIL, 128), BF16), ((TOK, 128), F32, 1), ((TOK, 128), F32, 1)],
+        [ANY] * 4,
+        [VMEM] * 3,
+        scratch=[
+            buf((TOK, WID), BF16),
+            buf((TOK, NST), BF16),
+            buf((HEADS, TOK), F32),
+            buf((HEADS, TOK), F32),
+            pltpu.SemaphoreType.DMA((4,)),
+        ],
         flops=1 << 29,
-    )(x, wr, step_size[0], log_decay[0])
+    )(far(x), far(wr), far(step_size[0].T), far(log_decay[0].T))
     ends = swap(pay, SEQ)
-    asks, place_col, place_row = call(
+    asks, place_col, place_row, live, tile_gain = call(
         places_body,
-        [((OWN, TAIL, 128), BF16), ((ROWS, 128), F32), ((8, ROWS), F32)],
+        [
+            ((OWN, TAIL, 128), BF16, 1),
+            ((ROWS, 128), F32, 1),
+            ((8, ROWS), F32, 1),
+            ((TILES, SLOTS), F32, 1),
+            ((TILES, FEAT), F32, 1),
+        ],
+        [VMEM] * 5,
+        [VMEM] * 5,
         flops=1 << 31,
-    )(block_list[0], depth)
+    )(block_list[0].T, depth_order[0].T, block_count, camera_index, view_gain[0].T)
     (local,) = call(
         fore_local_body,
-        [((TOK, WID), F32)],
-        scratch=[pltpu.VMEM((NST, WID), BF16)],
+        [((TOK, WID), F32, 1)],
+        [VMEM] * 5,
+        [VMEM],
+        scratch=[buf((NST, WID), BF16)],
         flops=1 << 32,
-    )(x, wr, rd, run, step)
-    (pay,) = call(prefix_body, [((OWN, NST + TAIL, 128), BF16)])(ends, asks)
+    )(x, wr, rd, held(run), held(step))
+    (pay,) = call(
+        prefix_body, [((OWN, NST + TAIL, 128), BF16)], [VMEM, VMEM], [VMEM]
+    )(ends, held(asks))
     states = swap(pay, SEQ)
     scan_out, answer = call(
-        features_body, [((TOK, WID), BF16), ((OWN, 128, FEAT), BF16)], flops=1 << 31
-    )(local, states, rd, run, head_weight)
+        features_body,
+        [((TOK, WID), BF16, 1), ((OWN, 128, FEAT), BF16)],
+        [VMEM] * 5,
+        [VMEM] * 2,
+        flops=1 << 31,
+    )(held(local), states, rd, held(run), head_weight)
     answered = swap(answer, SEQ)
     (outgoing,) = call(
         composite_body,
         [((OWN * 128, FEAT), BF16)],
+        [VMEM] * 6,
+        [VMEM],
         scratch=[
-            pltpu.VMEM((ROWS, FEAT), F32),
-            pltpu.VMEM((ROWS, 128), F32),
-            pltpu.VMEM((ROWS, 128), F32),
-            pltpu.VMEM((ROWS, FEAT), BF16),
+            buf((ROWS, FEAT), F32),
+            buf((ROWS, 128), F32),
+            buf((ROWS, 128), F32),
+            buf((ROWS, FEAT), BF16),
         ],
         flops=1 << 32,
     )(
         answered.reshape(OWN * 128, FEAT),
-        place_col,
-        place_row,
-        depth,
-        block_count[0][:, None],
-        camera_index[0][:, None],
-        view_gain[0],
+        held(place_col),
+        held(place_row),
+        held(live),
+        held(tile_gain),
         target_color[0],
     )
     homed = swap(outgoing.reshape(OWN, 128, FEAT), SEQ)
     out_grad, pay = call(
         token_grad_body,
-        [((TOK, WID), BF16), ((OWN, NST + FEAT, 128), BF16)],
-        in_specs=[vmem, tail_spec, vmem, vmem, vmem, vmem],
-        out_specs=[vmem, vmem],
+        [((TOK, WID), BF16, 1), ((OWN, NST + FEAT, 128), BF16)],
+        [VMEM, TAIL_SPEC, VMEM, VMEM, VMEM, VMEM],
+        [VMEM, VMEM],
         grid=(1,),
         flops=1 << 31,
-    )(homed.reshape(OWN * 128, FEAT), states, head_weight, scan_out, rd, run)
+    )(homed.reshape(OWN * 128, FEAT), states, head_weight, held(scan_out), rd, held(run))
     back = swap(pay, SEQ)
     (within,) = call(
         back_local_body,
-        [((TOK, WID), F32)],
-        scratch=[pltpu.VMEM((NST, WID), BF16)],
+        [((TOK, WID), F32, 1)],
+        [VMEM] * 4,
+        [VMEM],
+        scratch=[buf((NST, WID), BF16)],
         flops=1 << 32,
-    )(out_grad, wr, rd, run)
-    (scene_part,) = call(scene_sum_body, [((8, FEAT, 128), BF16)])(back)
-    scene_parts = swap(scene_part, ("dp",))
-    (pay,) = call(
+    )(held(out_grad), wr, rd, held(run))
+    pay, part = call(
         suffix_body,
-        [((OWN, NST + FEAT, 128), BF16)],
-        in_specs=[pl.BlockSpec((OWN, NST, 128), lambda *_: (0, 0, 0)), tail_spec],
-        out_specs=[pl.BlockSpec((OWN, NST, 128), lambda *_: (0, 0, 0))],
+        [((OWN, NST, 128), BF16), ((FEAT, 128), F32)],
+        [VMEM, TAIL_SPEC],
+        [VMEM, VMEM],
         grid=(1,),
     )(back, ends)
-    scale = 1.0 / np.sqrt(np.float64(lax.axis_size("dp") * TOK * lax.axis_size(SEQ)))
+    states_back = swap(pay, SEQ)
+    scenes = lax.axis_size("dp")
+    hop = 1
+    while hop < scenes:
+        part = part + lax.ppermute(part, "dp", [(i, i ^ hop) for i in range(scenes)])
+        hop *= 2
+    scale = np.float32(1.0 / np.sqrt(float(scenes * TOK * lax.axis_size(SEQ))))
     (pay,) = call(
-        lambda *refs: all_scenes_body(np.float32(scale), *refs),
-        [((OWN, NST + FEAT, 128), BF16)],
-        in_specs=[vmem, pl.BlockSpec(memory_space=pl.ANY)],
-        out_specs=[pl.BlockSpec((OWN, 128, 128), lambda i: (0, 1 + i, 0))],
-        grid=(2,),
-        alias={1: 0},
-    )(scene_parts, pay)
-    states_back = swap(pay, SEQ)
-    grad, wgrad = call(
-        input_grad_body, [((TOK, WID), BF16), ((WID, FEAT), F32)], flops=1 << 30
-    )(within, states_back, wr, run, step)
+        lambda *refs: spread_weight_body(scale, *refs),
+        [((OWN, 128, FEAT), BF16)],
+        [VMEM],
+        [VMEM],
+    )(part)
+    wgrad = swap(pay, SEQ).reshape(WID, FEAT).astype(F32)
+    (grad,) = call(
+        input_grad_body, [((TOK, WID), BF16)], [VMEM] * 5, [VMEM], flops=1 << 30
+    )(held(within), states_back, wr, held(run), held(step))
     return grad[None], wgrad
 
 

time: 166 us -> 152 us (0.916)
  waiting for transfers between devices: 58.5 us -> 34.9 us
  blocking collectives: 41.6 us -> 56.4 us
  local copies, waits for them, and re-layouts: 13.5 us -> 4.18 us
  starting transfers between devices: 23.9 us -> 27.4 us
  other arithmetic: 0 us -> 2.75 us
  Pallas kernels: 26.5 us -> 24.7 us
    all_to_all x5 -> x4, waiting for transfers between devices: 58.5 us -> 26.2 us  [swap(): return lax.all_to_all(x, axes, split_axis=0, concat_axis=0, tiled=True)]
    all_to_all x2 -> x3, blocking collectives: 41.6 us -> 56.4 us  [swap(): return lax.all_to_all(x, axes, split_axis=0, concat_axis=0, tiled=True)]
    unnamed x50 -> x27, local copies, waits for them, and re-layouts: 13.2 us -> 4.18 us
    ppermute x0 -> x3, waiting for transfers between devices: none -> 8.64 us  [shards(): lax.ppermute(part, 'dp', [(i, i ^ hop) for i in range(scenes)])]
    ppermute x0 -> x3, starting transfers between devices: none -> 4.96 us  [shards(): lax.ppermute(part, 'dp', [(i, i ^ hop) for i in range(scenes)])]
    convert_element_type x0 -> x1, other arithmetic: none -> 2.7 us  [shards(): wgrad = swap(pay, SEQ).reshape(WID, FEAT).astype(F32)]
    pallas_call x12 -> x11, Pallas kernels: 26.5 us -> 24.7 us  [the longest x1 4.26 us: shards(): call(fore_local_body, [((TOK, WID), F32, 1)], [VMEM] * 5, [VMEM], scratch...]
    all_to_all x5 -> x4, starting transfers between devices: 23.9 us -> 22.5 us  [swap(): return lax.all_to_all(x, axes, split_axis=0, concat_axis=0, tiled=True)]
  transfers between devices with their start and end apart: 5 -> 7, of which waited for: 5 -> 6; matrix products, arithmetic and copies ran while one was open for 0% -> 0% of each run, Pallas kernels for 6% -> 8%
where the time goes in v1:
time: 152 us; the launch traced here: 151 us
  blocking collectives  56.4 us (37%)
  waiting for transfers between devices  34.9 us (23%)
  starting transfers between devices  27.4 us (18%)
  Pallas kernels  24.7 us (16%)
  local copies, waits for them, and re-layouts  4.18 us (3%)
  other arithmetic  2.75 us (2%)
    all_to_all x3, blocking collectives, swap(): return lax.all_to_all(x, axes, split_axis=0, concat_axis=0, tiled=True)  56.4 us
    all_to_all x4, waiting for transfers between devices, swap(): return lax.all_to_all(x, axes, split_axis=0, concat_axis=0, tiled=True)  26.2 us
    all_to_all x4, starting transfers between devices, swap(): return lax.all_to_all(x, axes, split_axis=0, concat_axis=0, tiled=True)  22.5 us
    ppermute x3, waiting for transfers between devices, shards(): lax.ppermute(part, 'dp', [(i, i ^ hop) for i in range(scenes)])  8.64 us
    ppermute x3, starting transfers between devices, shards(): lax.ppermute(part, 'dp', [(i, i ^ hop) for i in range(scenes)])  4.96 us
    pallas_call x1, Pallas kernels, shards(): call(fore_local_body, [((TOK, WID), F32, 1)], [VMEM] * 5, [VMEM], scratch...  4.26 us
    unnamed x27, local copies, waits for them, and re-layouts  4.18 us
    pallas_call x1, Pallas kernels, shards(): call(composite_body, [((OWN * 128, FEAT), BF16)], [VMEM] * 6, [VMEM], scr...  3.12 us
  transfers between devices with their start and end apart: 7, of which 6 were waited for; matrix products, arithmetic and copies ran while one was open for 0% of the time, Pallas kernels for 8%

profile of v1, /device:TPU:0, one launch (start us, length us, event | category | flops | bytes accessed | tf_op | source)
XLA Modules:
  0.0 151.2 jit_solution(13004662568169581972)
XLA Ops:
  0.7 3.0 %shard_map.131 = (bf16[16,144,128]{2,1,0:T(8,128)(2,1)}, f32[256,128]{1,0:T(8,128)S(1)}, f32[256,128]{1,0:T(8,128)S(1)}) custom-call(bf16[256,2048]{1,0:T(8,128)(2,1)} %bitcast.36, bf16[256,128]{1,0:T(8,128)(2,1)} %bitcast.31, f32[64,256]{1,0:T(8,128)} %bitcast.46, f32[64,256]{1,0:T(8,128)} %bitcast.47), custom_call_target="tpu_custom_call" | custom-call | flops 536870912 | bytes 4194304 | tf_op jit(solution)/shard_map/pallas_call | solution.py:456
  3.7 8.0 %all-to-all-start = ((bf16[16,144,128]{2,1,0:T(8,128)(2,1)}), bf16[16,144,128]{2,1,0:T(8,128)(2,1)S(1)}, u32[]{:S(2)}, u32[]{:S(2)}) async-start(bf16[16,144,128]{2,1,0:T(8,128)(2,1)} %get-tuple-element.18), calls=%async_computation | async-start | bytes 1179648 | tf_op jit(solution)/shard_map/all_to_all | solution.py:436
  11.8 1.4 shard_map.133
  13.2 0.0 copy-start
  13.2 10.4 %all-to-all-done.got.tails = bf16[16,144,128]{2,1,0:T(8,128)(2,1)S(1)} async-done(((bf16[16,144,128]{2,1,0:T(8,128)(2,1)}), bf16[16,144,128]{2,1,0:T(8,128)(2,1)S(1)}, u32[]{:S(2)}, u32[]{:S(2)}) %all-to-all-start) | async-done | bytes 589856 | tf_op jit(solution)/shard_map/all_to_all | solution.py:436
  23.6 1.0 shard_map.134
  24.6 3.8 %all-to-all-start.1 = ((bf16[16,144,128]{2,1,0:T(8,128)(2,1)}), bf16[16,144,128]{2,1,0:T(8,128)(2,1)S(1)}, u32[]{:S(2)}, u32[]{:S(2)}) async-start(bf16[16,144,128]{2,1,0:T(8,128)(2,1)} %shard_map.134), calls=%async_computation.1 | async-start | bytes 1179648 | tf_op jit(solution)/shard_map/all_to_all | solution.py:436
  28.4 4.3 %shard_map.132.local = f32[256,2048]{1,0:T(8,128)S(1)} custom-call(bf16[256,2048]{1,0:T(8,128)(2,1)S(1)} %bitcast.37, bf16[256,128]{1,0:T(8,128)(2,1)S(1)} %bitcast.32, bf16[256,128]{1,0:T(8,128)(2,1)S(1)} %bitcast.39, f32[256,128]{1,0:T(8,128)S(1)} %get-tuple-element.16.run, f32[256,128]{1,0:T(8,128)S(1)} %get-tuple-element.17.step), custom_call_target="tpu_custom_call" | custom-call | flops 4294967296 | bytes 4194304 | tf_op jit(solution)/shard_map/pallas_call | solution.py:484
  32.7 1.3 copy-done.10
  34.0 5.4 %all-to-all-done.1.got.asked = bf16[16,144,128]{2,1,0:T(8,128)(2,1)S(1)} async-done(((bf16[16,144,128]{2,1,0:T(8,128)(2,1)}), bf16[16,144,128]{2,1,0:T(8,128)(2,1)S(1)}, u32[]{:S(2)}, u32[]{:S(2)}) %all-to-all-start.1) | async-done | bytes 589856 | tf_op jit(solution)/shard_map/all_to_all | solution.py:436
  39.4 1.2 copy-done.2
  40.7 1.6 %copy-done.11 = f32[256,2048]{1,0:T(8,128)S(1)} copy-done((f32[256,2048]{1,0:T(8,128)S(1)}, f32[256,2048]{1,0:T(8,128)}, u32[]{:S(2)}) %copy-start.11) | copy-done | bytes 2097176
  42.2 1.8 %shard_map.135 = (bf16[256,2048]{1,0:T(8,128)(2,1)S(1)}, bf16[16,128,256]{2,1,0:T(8,128)(2,1)S(1)}) custom-call(f32[256,2048]{1,0:T(8,128)S(1)} %copy-done.11, bf16[16,144,128]{2,1,0:T(8,128)(2,1)S(1)} %all-to-all-done.1.got.asked, bf16[256,128]{1,0:T(8,128)(2,1)S(1)} %bitcast.40, f32[256,128]{1,0:T(8,128)S(1)} %get-tuple-element.16.run, ...), custom_call_target="tpu_custom_call" | custom-call | flops 2147483648 | bytes 4194304 | tf_op jit(solution)/shard_map/pallas_call | solution.py:496
  44.1 18.2 %all_to_all.35 = bf16[16,128,256]{2,1,0:T(8,128)(2,1)S(1)} all-to-all(bf16[16,128,256]{2,1,0:T(8,128)(2,1)S(1)} %get-tuple-element.20), channel_id=1, replica_groups=mesh['dp'=8,'seq_0'=4,'seq_1'=4] {'seq_0','seq_1'}, dimensions={0} | all-to-all | bytes 2097152 | tf_op jit(solution)/shard_map/all_to_all | solution.py:436
  62.2 3.1 %shard_map.136 = bf16[2048,256]{1,0:T(8,128)(2,1)S(1)} custom-call(bf16[2048,256]{1,0:T(8,128)(2,1)S(1)} %bitcast.28, f32[1024,128]{1,0:T(8,128)S(1)} %get-tuple-element.21.place_col, f32[8,1024]{1,0:T(8,128)S(1)} %get-tuple-element.22.place_row, f32[64,16]{1,0:T(8,128)S(1)} %get-tuple-element.23.live, f32[64,256]{1,0:T(8,128)S(1)} %get-tuple-element.24.tile_gain, ...), custom_call_target="tpu_custom_call" | custom-call | flops 4294967296 | bytes 4194304 | tf_op jit(solution)/shard_map/pallas_call | solution.py:504
  65.4 17.0 %all_to_all.36 = bf16[16,128,256]{2,1,0:T(8,128)(2,1)S(1)} all-to-all(bf16[16,128,256]{2,1,0:T(8,128)(2,1)S(1)} %bitcast.30), channel_id=1, replica_groups=mesh['dp'=8,'seq_0'=4,'seq_1'=4] {'seq_0','seq_1'}, dimensions={0} | all-to-all | bytes 2097152 | tf_op jit(solution)/shard_map/all_to_all | solution.py:436
  82.3 2.9 %shard_map.137 = (bf16[256,2048]{1,0:T(8,128)(2,1)S(1)}, bf16[16,384,128]{2,1,0:T(8,128)(2,1)S(1)}) custom-call(bf16[2048,256]{1,0:T(8,128)(2,1)S(1)} %bitcast.29, bf16[16,144,128]{2,1,0:T(8,128)(2,1)S(1)} %all-to-all-done.1.got.asked, bf16[2048,256]{1,0:T(8,128)(2,1)S(1)} %copy-done.3, bf16[256,2048]{1,0:T(8,128)(2,1)S(1)} %get-tuple-element.25.scan_out, ...), custom_call_target="tpu_custom_call" | custom-call | flops 2147483648 | bytes 4194304 | tf_op jit(solution)/shard_map/pallas_call | solution.py:525
  85.3 21.2 %all_to_all.37.got = bf16[16,384,128]{2,1,0:T(8,128)(2,1)S(1)} all-to-all(bf16[16,384,128]{2,1,0:T(8,128)(2,1)S(1)} %get-tuple-element.27), channel_id=1, replica_groups=mesh['dp'=8,'seq_0'=4,'seq_1'=4] {'seq_0','seq_1'}, dimensions={0} | all-to-all | bytes 3145728 | tf_op jit(solution)/shard_map/all_to_all | solution.py:436
  106.5 1.0 shard_map.139
  107.5 3.6 %all-to-all-start.5 = ((bf16[16,128,128]{2,1,0:T(8,128)(2,1)}), bf16[16,128,128]{2,1,0:T(8,128)(2,1)S(1)}, u32[]{:S(2)}, u32[]{:S(2)}) async-start(bf16[16,128,128]{2,1,0:T(8,128)(2,1)} %get-tuple-element.28), calls=%async_computation.5 | async-start | bytes 1048576 | tf_op jit(solution)/shard_map/all_to_all | solution.py:436
  111.0 0.1 collective-permute-start
  111.1 1.3 collective-permute-done
  112.5 1.6 %collective-permute-start.1 = (f32[256,128]{1,0:T(8,128)S(1)}, f32[256,128]{1,0:T(8,128)S(1)}, u32[]{:S(2)}, u32[]{:S(2)}) collective-permute-start(f32[256,128]{1,0:T(8,128)S(1)} %add.9), channel_id=1, source_target_pairs={{0,32},{16,48},{32,0},{48,16},{64,96},{80,112},{96,64},{112,80},{1... | collective-permute-start | bytes 393224 | tf_op jit(solution)/shard_map/ppermute | solution.py:553
  114.1 4.0 %collective-permute-done.1 = f32[256,128]{1,0:T(8,128)S(1)} collective-permute-done((f32[256,128]{1,0:T(8,128)S(1)}, f32[256,128]{1,0:T(8,128)S(1)}, u32[]{:S(2)}, u32[]{:S(2)}) %collective-permute-start.1) | collective-permute-done | bytes 131104 | tf_op jit(solution)/shard_map/ppermute | solution.py:553
  118.1 3.2 %collective-permute-start.2 = (f32[256,128]{1,0:T(8,128)S(1)}, f32[256,128]{1,0:T(8,128)S(1)}, u32[]{:S(2)}, u32[]{:S(2)}) collective-permute-start(f32[256,128]{1,0:T(8,128)S(1)} %add.10), channel_id=1, source_target_pairs={{0,64},{16,80},{32,96},{48,112},{64,0},{80,16},{96,32},{112,48},{1... | collective-permute-start | bytes 393224 | tf_op jit(solution)/shard_map/ppermute | solution.py:553
  121.4 3.3 %collective-permute-done.2 = f32[256,128]{1,0:T(8,128)S(1)} collective-permute-done((f32[256,128]{1,0:T(8,128)S(1)}, f32[256,128]{1,0:T(8,128)S(1)}, u32[]{:S(2)}, u32[]{:S(2)}) %collective-permute-start.2) | collective-permute-done | bytes 131104 | tf_op jit(solution)/shard_map/ppermute | solution.py:553
  124.7 1.1 shard_map.141
  125.9 7.1 %all-to-all-start.6 = ((bf16[16,128,256]{2,1,0:T(8,128)(2,1)}), bf16[16,128,256]{2,1,0:T(8,128)(2,1)}, u32[]{:S(2)}, u32[]{:S(2)}) async-start(bf16[16,128,256]{2,1,0:T(8,128)(2,1)} %shard_map.141), calls=%async_computation.6 | async-start | bytes 2097152 | tf_op jit(solution)/shard_map/all_to_all | solution.py:436
  133.0 3.1 %shard_map.138.within = f32[256,2048]{1,0:T(8,128)S(1)} custom-call(bf16[256,2048]{1,0:T(8,128)(2,1)S(1)} %get-tuple-element.26.og, bf16[256,128]{1,0:T(8,128)(2,1)S(1)} %bitcast.33, bf16[256,128]{1,0:T(8,128)(2,1)S(1)} %bitcast.42, f32[256,128]{1,0:T(8,128)S(1)} %get-tuple-element.16.run), custom_call_target="tpu_custom_call" | custom-call | flops 4294967296 | bytes 4194304 | tf_op jit(solution)/shard_map/pallas_call | solution.py:534
  136.1 2.0 %shard_map.140 = bf16[256,2048]{1,0:T(8,128)(2,1)} custom-call(f32[256,2048]{1,0:T(8,128)S(1)} %shard_map.138.within, bf16[16,128,128]{2,1,0:T(8,128)(2,1)S(1)} %all-to-all-done.5.got, bf16[256,128]{1,0:T(8,128)(2,1)S(1)} %bitcast.34, f32[256,128]{1,0:T(8,128)S(1)} %get-tuple-element.16.run, f32[256,128]{1,0:T(8,128)S(1)} %get-tuple-element.17.step), custom_call_target="tpu_custom_call" | custom-call | flops 1073741824 | bytes 4194304 | tf_op jit(solution)/shard_map/pallas_call | solution.py:563
  138.1 10.4 %all-to-all-done.6 = bf16[16,128,256]{2,1,0:T(8,128)(2,1)} async-done(((bf16[16,128,256]{2,1,0:T(8,128)(2,1)}), bf16[16,128,256]{2,1,0:T(8,128)(2,1)}, u32[]{:S(2)}, u32[]{:S(2)}) %all-to-all-start.6) | async-done | bytes 1048608 | tf_op jit(solution)/shard_map/all_to_all | solution.py:436
  148.5 2.7 %bitcast_convert_fusion = f32[2048,256]{1,0:T(8,128)} fusion(bf16[16,128,256]{2,1,0:T(8,128)(2,1)} %all-to-all-done.6), kind=kLoop, calls=%fused_computation | loop fusion | flops 524288 | bytes 3145728 | tf_op jit(solution)/shard_map/convert_element_type | solution.py:562
  (27 shorter events, 0.1 us)
Async XLA Ops:
  0.6 11.1 %copy-start.12 = (f32[1,8,3]{1,0,2:T(1,128)S(1)}, f32[1,8,3]{1,0,2:T(1,128)}, u32[]{:S(2)}) copy-start(f32[1,8,3]{1,0,2:T(1,128)} %param.22) | copy-start | bytes 292
  0.6 11.1 %copy-start.9 = (s32[1,64]{1,0:T(1,128)S(1)}, s32[1,64]{1,0:T(1,128)}, u32[]{:S(2)}) copy-start(s32[1,64]{1,0:T(1,128)} %camera.1) | copy-start | bytes 772
  0.7 11.1 %copy-start.7 = (s32[1,64,16]{1,2,0:T(8,128)S(1)}, s32[1,64,16]{1,2,0:T(8,128)}, u32[]{:S(2)}) copy-start(s32[1,64,16]{1,2,0:T(8,128)} %param.20) | copy-start | bytes 12292
  0.7 11.1 %copy-start.8 = (s32[1,64]{1,0:T(1,128)S(1)}, s32[1,64]{1,0:T(1,128)}, u32[]{:S(2)}) copy-start(s32[1,64]{1,0:T(1,128)} %count.1) | copy-start | bytes 772
  0.7 11.1 %copy-start.6 = (s32[1,64,16]{1,2,0:T(8,128)S(1)}, s32[1,64,16]{1,2,0:T(8,128)}, u32[]{:S(2)}) copy-start(s32[1,64,16]{1,2,0:T(8,128)} %param.18) | copy-start | bytes 12292
  3.7 19.9 %all-to-all-start = ((bf16[16,144,128]{2,1,0:T(8,128)(2,1)}), bf16[16,144,128]{2,1,0:T(8,128)(2,1)S(1)}, u32[]{:S(2)}, u32[]{:S(2)}) async-start(bf16[16,144,128]{2,1,0:T(8,128)(2,1)} %get-tuple-element.18), calls=%async_computation | async-start | bytes 1179648 | tf_op jit(solution)/shard_map/all_to_all | solution.py:436
  13.2 15.2 %copy-start = (bf16[1,256,128]{2,1,0:T(8,128)(2,1)S(1)}, bf16[1,256,128]{2,1,0:T(8,128)(2,1)}, u32[]{:S(2)}) copy-start(bf16[1,256,128]{2,1,0:T(8,128)(2,1)} %param.13) | copy-start | bytes 196612
  13.2 15.2 %copy-start.1 = (bf16[1,256,2048]{2,1,0:T(8,128)(2,1)S(1)}, bf16[1,256,2048]{2,1,0:T(8,128)(2,1)}, u32[]{:S(2)}) copy-start(bf16[1,256,2048]{2,1,0:T(8,128)(2,1)} %param.12) | copy-start | bytes 3145732
  13.2 15.2 %copy-start.5 = (bf16[1,256,128]{2,1,0:T(8,128)(2,1)S(1)}, bf16[1,256,128]{2,1,0:T(8,128)(2,1)}, u32[]{:S(2)}) copy-start(bf16[1,256,128]{2,1,0:T(8,128)(2,1)} %param.14) | copy-start | bytes 196612
  24.6 14.9 %all-to-all-start.1 = ((bf16[16,144,128]{2,1,0:T(8,128)(2,1)}), bf16[16,144,128]{2,1,0:T(8,128)(2,1)S(1)}, u32[]{:S(2)}, u32[]{:S(2)}) async-start(bf16[16,144,128]{2,1,0:T(8,128)(2,1)} %shard_map.134), calls=%async_computation.1 | async-start | bytes 1179648 | tf_op jit(solution)/shard_map/all_to_all | solution.py:436
  32.7 1.3 copy-start.10
  39.4 1.2 copy-start.2
  40.7 1.6 %copy-start.11 = (f32[256,2048]{1,0:T(8,128)S(1)}, f32[256,2048]{1,0:T(8,128)}, u32[]{:S(2)}) copy-start(f32[256,2048]{1,0:T(8,128)} %copy-done.10) | copy-start | bytes 6291460
  44.0 18.2 %copy-start.4 = (f32[1,64,192]{2,1,0:T(8,128)S(1)}, f32[1,64,192]{2,1,0:T(8,128)}, u32[]{:S(2)}) copy-start(f32[1,64,192]{2,1,0:T(8,128)} %param.23) | copy-start | bytes 147460
  65.4 17.0 %copy-start.3 = (bf16[2048,256]{1,0:T(8,128)(2,1)S(1)}, bf16[2048,256]{1,0:T(8,128)(2,1)}, u32[]{:S(2)}) copy-start(bf16[2048,256]{1,0:T(8,128)(2,1)} %weight.3) | copy-start | bytes 3145732
  107.5 18.4 %all-to-all-start.5 = ((bf16[16,128,128]{2,1,0:T(8,128)(2,1)}), bf16[16,128,128]{2,1,0:T(8,128)(2,1)S(1)}, u32[]{:S(2)}, u32[]{:S(2)}) async-start(bf16[16,128,128]{2,1,0:T(8,128)(2,1)} %get-tuple-element.28), calls=%async_computation.5 | async-start | bytes 1048576 | tf_op jit(solution)/shard_map/all_to_all | solution.py:436
  111.0 1.4 collective-permute-start
  112.5 5.6 %collective-permute-start.1 = (f32[256,128]{1,0:T(8,128)S(1)}, f32[256,128]{1,0:T(8,128)S(1)}, u32[]{:S(2)}, u32[]{:S(2)}) collective-permute-start(f32[256,128]{1,0:T(8,128)S(1)} %add.9), channel_id=1, source_target_pairs={{0,32},{16,48},{32,0},{48,16},{64,96},{80,112},{96,64},{112,80},{1... | collective-permute-start | bytes 393224 | tf_op jit(solution)/shard_map/ppermute | solution.py:553
  118.1 6.6 %collective-permute-start.2 = (f32[256,128]{1,0:T(8,128)S(1)}, f32[256,128]{1,0:T(8,128)S(1)}, u32[]{:S(2)}, u32[]{:S(2)}) collective-permute-start(f32[256,128]{1,0:T(8,128)S(1)} %add.10), channel_id=1, source_target_pairs={{0,64},{16,80},{32,96},{48,112},{64,0},{80,16},{96,32},{112,48},{1... | collective-permute-start | bytes 393224 | tf_op jit(solution)/shard_map/ppermute | solution.py:553
  125.9 22.6 %all-to-all-start.6 = ((bf16[16,128,256]{2,1,0:T(8,128)(2,1)}), bf16[16,128,256]{2,1,0:T(8,128)(2,1)}, u32[]{:S(2)}, u32[]{:S(2)}) async-start(bf16[16,128,256]{2,1,0:T(8,128)(2,1)} %shard_map.141), calls=%async_computation.6 | async-start | bytes 2097152 | tf_op jit(solution)/shard_map/all_to_all | solution.py:436

commit v2 on v1

--- a/solution.py
+++ b/solution.py
@@ -25,7 +25,7 @@
 TILES = 64
 SLOTS = 16
 ROWS = TILES * SLOTS
-TAIL = 16
+TAIL = 8
 
 
 def dot(a, b):
@@ -63,11 +63,11 @@
 
 ANY = pl.BlockSpec(memory_space=pl.ANY)
 VMEM = pl.BlockSpec(memory_space=pltpu.VMEM)
+SMEM = pl.BlockSpec(memory_space=pltpu.SMEM)
 TAIL_SPEC = pl.BlockSpec((OWN, TAIL, 128), lambda *_: (0, NST // TAIL, 0))
 
 
-def near(shape, dtype):
-    return pltpu.VMEM(shape, dtype)
+PLACES = (pltpu.HBM, pltpu.VMEM)
 
 
 def held(x):
@@ -82,7 +82,8 @@
     return pl.pallas_call(
         body,
         out_shape=[
-            (near if len(o) == 3 else jax.ShapeDtypeStruct)(o[0], o[1]) for o in outs
+            (PLACES[o[2]] if len(o) == 3 else jax.ShapeDtypeStruct)(o[0], o[1])
+            for o in outs
         ],
         grid_spec=pl.GridSpec(
             grid=grid, in_specs=ins, out_specs=out_specs, scratch_shapes=list(scratch)
@@ -93,7 +94,7 @@
 
 
 def local_end_body(
-    x_far, wr_far, step_far, logd_far, pay, run_out, step_out, x, wr, step, logd, sem
+    core, x_far, wr_far, step_far, logd_far, pay, run_out, step_out, x, wr, step, logd, sem
 ):
     moves = [
         pltpu.make_async_copy(a, b, sem.at[k])
@@ -101,6 +102,7 @@
             ((logd_far, logd), (step_far, step), (wr_far, wr), (x_far, x))
         )
     ]
+    del core
     for m in moves:
         m.start()
     moves[0].wait()
@@ -144,7 +146,8 @@
     )
 
 
-def prefix_body(got, asks, pay):
+def prefix_body(got, asks, local, pay):
+    del local
     state = jnp.zeros((NST, 128), F32)
     for d in range(OWN):
         pay[d, 0:NST, :] = state.astype(BF16)
@@ -373,6 +376,7 @@
 
 
 GAUSS_LANES = 64
+HALF = 128
 
 
 def token_grad_body(homed, asked, weight, scan_out, rd, run, out_grad, pay):
@@ -402,22 +406,33 @@
             pay[2 * c + k, NST : NST + FEAT, :] = part[:, lanes]
 
 
-def suffix_body(got, tails, pay, part):
-    state = jnp.zeros((NST, 128), F32)
-    for d in reversed(range(OWN)):
-        pay[d] = state.astype(BF16)
-        if d > 0:
-            state = decayed(tails[d]) * state + got[d, 0:NST, :].astype(F32)
+def scene_sum_body(core, got, mine, theirs):
     total = jnp.zeros((FEAT, 128), F32)
     for d in range(OWN):
         total = total + got[d, NST : NST + FEAT, :].astype(F32)
-    part[...] = total
-
-
-def spread_weight_body(scale, part, pay):
+    first = core[0] == 0
+    mine[...] = jnp.where(first, total[0:HALF, :], total[HALF:FEAT, :])
+    theirs[...] = jnp.where(first, total[HALF:FEAT, :], total[0:HALF, :])
+
+
+def suffix_body(scale, got, tails, part, within, pay):
+    del within
+    state = jnp.zeros((NST, 128), F32)
     block = (part[...] * scale).T.astype(BF16)
+    for d in reversed(range(OWN)):
+        pay[d, 0:NST, :] = state.astype(BF16)
+        pay[d, NST : NST + HALF, :] = block
+        if d > 0:
+            state = decayed(tails[d]) * state + got[d].astype(F32)
+
+
+def join_weight_body(core, own, other, out):
+    first = core[0] == 0
     for d in range(OWN):
-        pay[d] = block
+        rows = slice(d * 128, (d + 1) * 128)
+        a, b = own[d, NST : NST + HALF, :].astype(F32), other[d].astype(F32)
+        out[rows, 0:HALF] = jnp.where(first, a, b)
+        out[rows, HALF:FEAT] = jnp.where(first, b, a)
 
 
 def input_grad_body(within, got, wr, run, step, grad):
@@ -427,7 +442,7 @@
     steps = split_pair(step[...])
     for c in range(NCH):
         e = spread_of(base, c)
-        state = jnp.concatenate([got[2 * c], got[2 * c + 1]], axis=1)
+        state = jnp.concatenate([got[2 * c, 0:NST, :], got[2 * c + 1, 0:NST, :]], axis=1)
         rows = within[:, cols(c)] + dot(tail, e) * dot(wr[...], state)
         grad[:, cols(c)] = (rows * dot(steps, e)).astype(BF16)
 
@@ -452,11 +467,17 @@
 ):
     x, wr, rd = ssm_input[0], write_basis[0], read_basis[0]
     buf = pltpu.VMEM
+    scenes = lax.axis_size("dp")
+    core = lax.axis_index("dp") % 2
+    core_ref = core.astype(jnp.int32).reshape(1)
+
+    def trade(v, hop):
+        return lax.ppermute(v, "dp", [(i, i ^ hop) for i in range(scenes)])
 
     pay, run, step = call(
         local_end_body,
         [((OWN, NST + TAIL, 128), BF16), ((TOK, 128), F32, 1), ((TOK, 128), F32, 1)],
-        [ANY] * 4,
+        [SMEM] + [ANY] * 4,
         [VMEM] * 3,
         scratch=[
             buf((TOK, WID), BF16),
@@ -466,16 +487,16 @@
             pltpu.SemaphoreType.DMA((4,)),
         ],
         flops=1 << 29,
-    )(far(x), far(wr), far(step_size[0].T), far(log_decay[0].T))
+    )(core_ref, far(x), far(wr), far(step_size[0].T), far(log_decay[0].T))
     ends = swap(pay, SEQ)
     asks, place_col, place_row, live, tile_gain = call(
         places_body,
         [
             ((OWN, TAIL, 128), BF16, 1),
-            ((ROWS, 128), F32, 1),
-            ((8, ROWS), F32, 1),
-            ((TILES, SLOTS), F32, 1),
-            ((TILES, FEAT), F32, 1),
+            ((ROWS, 128), F32, 0),
+            ((8, ROWS), F32, 0),
+            ((TILES, SLOTS), F32, 0),
+            ((TILES, FEAT), F32, 0),
         ],
         [VMEM] * 5,
         [VMEM] * 5,
@@ -483,15 +504,15 @@
     )(block_list[0].T, depth_order[0].T, block_count, camera_index, view_gain[0].T)
     (local,) = call(
         fore_local_body,
-        [((TOK, WID), F32, 1)],
+        [((TOK, WID), F32, 0)],
         [VMEM] * 5,
         [VMEM],
         scratch=[buf((NST, WID), BF16)],
         flops=1 << 32,
     )(x, wr, rd, held(run), held(step))
     (pay,) = call(
-        prefix_body, [((OWN, NST + TAIL, 128), BF16)], [VMEM, VMEM], [VMEM]
-    )(ends, held(asks))
+        prefix_body, [((OWN, NST + TAIL, 128), BF16)], [VMEM, VMEM, ANY], [VMEM]
+    )(ends, held(asks), far(local))
     states = swap(pay, SEQ)
     scan_out, answer = call(
         features_body,
@@ -499,7 +520,7 @@
         [VMEM] * 5,
         [VMEM] * 2,
         flops=1 << 31,
-    )(held(local), states, rd, held(run), head_weight)
+    )(local, states, rd, held(run), head_weight)
     answered = swap(answer, SEQ)
     (outgoing,) = call(
         composite_body,
@@ -515,10 +536,10 @@
         flops=1 << 32,
     )(
         answered.reshape(OWN * 128, FEAT),
-        held(place_col),
-        held(place_row),
-        held(live),
-        held(tile_gain),
+        place_col,
+        place_row,
+        live,
+        tile_gain,
         target_color[0],
     )
     homed = swap(outgoing.reshape(OWN, 128, FEAT), SEQ)
@@ -539,30 +560,30 @@
         scratch=[buf((NST, WID), BF16)],
         flops=1 << 32,
     )(held(out_grad), wr, rd, held(run))
-    pay, part = call(
-        suffix_body,
-        [((OWN, NST, 128), BF16), ((FEAT, 128), F32)],
-        [VMEM, TAIL_SPEC],
-        [VMEM, VMEM],
-        grid=(1,),
-    )(back, ends)
-    states_back = swap(pay, SEQ)
-    scenes = lax.axis_size("dp")
-    hop = 1
+    mine, theirs = call(
+        scene_sum_body, [((HALF, 128), F32)] * 2, [SMEM, VMEM], [VMEM] * 2
+    )(core_ref, back)
+    part = mine + trade(theirs, 1)
+    hop = 2
     while hop < scenes:
-        part = part + lax.ppermute(part, "dp", [(i, i ^ hop) for i in range(scenes)])
+        part = part + trade(part, hop)
         hop *= 2
     scale = np.float32(1.0 / np.sqrt(float(scenes * TOK * lax.axis_size(SEQ))))
     (pay,) = call(
-        lambda *refs: spread_weight_body(scale, *refs),
-        [((OWN, 128, FEAT), BF16)],
+        lambda *refs: suffix_body(scale, *refs),
+        [((OWN, NST + HALF, 128), BF16)],
+        [pl.BlockSpec((OWN, NST, 128), lambda *_: (0, 0, 0)), TAIL_SPEC, VMEM, ANY],
         [VMEM],
-        [VMEM],
-    )(part)
-    wgrad = swap(pay, SEQ).reshape(WID, FEAT).astype(F32)
+        grid=(1,),
+    )(back, ends, part, within)
+    last = swap(pay, SEQ)
+    other = trade(last[:, NST:, :], 1)
     (grad,) = call(
         input_grad_body, [((TOK, WID), BF16)], [VMEM] * 5, [VMEM], flops=1 << 30
-    )(held(within), states_back, wr, held(run), held(step))
+    )(held(within), last, wr, held(run), held(step))
+    (wgrad,) = call(
+        join_weight_body, [((WID, FEAT), F32)], [SMEM, VMEM, VMEM], [VMEM]
+    )(core_ref, last, other)
     return grad[None], wgrad
 
 

time: 152 us -> 140 us (0.921)
  blocking collectives: 56.4 us -> 90.5 us
  waiting for transfers between devices: 34.9 us -> 7.8 us
  starting transfers between devices: 27.4 us -> 13.1 us
  local copies, waits for them, and re-layouts: 4.18 us -> 0.11 us
  other arithmetic: 2.75 us -> 0.03 us
    all_to_all x3 -> x5, blocking collectives: 56.4 us -> 90.5 us  [swap(): return lax.all_to_all(x, axes, split_axis=0, concat_axis=0, tiled=True)]
    all_to_all x4 -> x1, waiting for transfers between devices: 26.2 us -> 3.89 us  [swap(): return lax.all_to_all(x, axes, split_axis=0, concat_axis=0, tiled=True)]
    all_to_all x4 -> x1, starting transfers between devices: 22.5 us -> 7.97 us  [swap(): return lax.all_to_all(x, axes, split_axis=0, concat_axis=0, tiled=True)]
    ppermute x3 -> x4, waiting for transfers between devices: 8.64 us -> 3.91 us  [trade(): return lax.ppermute(v, 'dp', [(i, i ^ hop) for i in range(scenes)])]
    unnamed x27 -> x31, local copies, waits for them, and re-layouts: 4.18 us -> 0.07 us
    convert_element_type x1 -> x0, other arithmetic: 2.7 us -> none  [shards(): wgrad = swap(pay, SEQ).reshape(WID, FEAT).astype(F32)]
    pallas_call x5 -> x6, Pallas kernels: 8.73 us -> 9.52 us  [the longest x1 5.6 us: shards(): call(fore_local_body, [((TOK, WID), F32, 0)], [VMEM] * 5, [VMEM], scratch...]
    ppermute x3 -> x4, starting transfers between devices: 4.96 us -> 5.09 us  [trade(): return lax.ppermute(v, 'dp', [(i, i ^ hop) for i in range(scenes)])]
  transfers between devices with their start and end apart: 7 -> 5, of which waited for: 6 -> 3; matrix products, arithmetic and copies ran while one was open for 0% -> 0% of each run, Pallas kernels for 8% -> 9%
where the time goes in v2:
time: 140 us; the launch traced here: 138 us
  blocking collectives  90.5 us (65%)
  Pallas kernels  25.5 us (18%)
  starting transfers between devices  13.1 us (9%)
  waiting for transfers between devices  7.8 us (6%)
    all_to_all x5, blocking collectives, swap(): return lax.all_to_all(x, axes, split_axis=0, concat_axis=0, tiled=True)  90.5 us
    all_to_all x1, starting transfers between devices, swap(): return lax.all_to_all(x, axes, split_axis=0, concat_axis=0, tiled=True)  7.97 us
    pallas_call x1, Pallas kernels, shards(): call(fore_local_body, [((TOK, WID), F32, 0)], [VMEM] * 5, [VMEM], scratch...  5.6 us
    ppermute x4, starting transfers between devices, trade(): return lax.ppermute(v, 'dp', [(i, i ^ hop) for i in range(scenes)])  5.09 us
    ppermute x4, waiting for transfers between devices, trade(): return lax.ppermute(v, 'dp', [(i, i ^ hop) for i in range(scenes)])  3.91 us
    all_to_all x1, waiting for transfers between devices, swap(): return lax.all_to_all(x, axes, split_axis=0, concat_axis=0, tiled=True)  3.89 us
    pallas_call x1, Pallas kernels, shards(): call(composite_body, [((OWN * 128, FEAT), BF16)], [VMEM] * 6, [VMEM], scr...  3.12 us
    pallas_call x1, Pallas kernels, shards(): call(back_local_body, [((TOK, WID), F32, 1)], [VMEM] * 4, [VMEM], scratch...  3.12 us
  transfers between devices with their start and end apart: 5, of which 3 were waited for; matrix products, arithmetic and copies ran while one was open for 0% of the time, Pallas kernels for 9%

profile of v2, /device:TPU:0, one launch (start us, length us, event | category | flops | bytes accessed | tf_op | source)
XLA Modules:
  0.0 137.9 jit_solution(3307709613407591453)
XLA Ops:
  0.6 0.0 copy-start.14
  0.7 3.0 %shard_map.131 = (bf16[16,136,128]{2,1,0:T(8,128)(2,1)}, f32[256,128]{1,0:T(8,128)S(1)}, f32[256,128]{1,0:T(8,128)S(1)}) custom-call(s32[1]{0:T(128)} %bitcast.3.core, bf16[256,2048]{1,0:T(8,128)(2,1)} %bitcast.34, bf16[256,128]{1,0:T(8,128)(2,1)} %bitcast.29, f32[64,256]{1,0:T(8,128)} %bitcast.44, f32[64,256]{1,0:T(8,128)} %bitcast.45), custom_call_target="tpu_custom_call" | custom-call | flops 536870912 | bytes 4194304 | tf_op jit(solution)/shard_map/pallas_call | solution.py:477
  3.7 8.0 %all-to-all-start = ((bf16[16,136,128]{2,1,0:T(8,128)(2,1)}), bf16[16,136,128]{2,1,0:T(8,128)(2,1)S(1)}, u32[]{:S(2)}, u32[]{:S(2)}) async-start(bf16[16,136,128]{2,1,0:T(8,128)(2,1)} %get-tuple-element.18), calls=%async_computation | async-start | bytes 1114112 | tf_op jit(solution)/shard_map/all_to_all | solution.py:451
  11.8 0.0 copy-start.1
  11.8 0.0 copy-start.2
  11.8 0.0 copy-start.5
  11.8 1.9 %shard_map.133 = (bf16[16,8,128]{2,1,0:T(8,128)(2,1)S(1)}, f32[1024,128]{1,0:T(8,128)}, f32[8,1024]{1,0:T(8,128)}, f32[64,16]{1,0:T(8,128)}, f32[64,256]{1,0:T(8,128)}) custom-call(s32[16,64]{1,0:T(8,128)S(1)} %bitcast.41, s32[16,64]{1,0:T(8,128)S(1)} %bitcast.42, s32[1,64]{1,0:T(1,128)S(1)} %copy-done.8, s32[1,64]{1,0:T(1,128)S(1)} %copy-done.9, ...), custom_call_target="tpu_custom_call" | custom-call | flops 2147483648 | bytes 4194304 | tf_op jit(solution)/shard_map/pallas_call | solution.py:492
  13.8 5.6 %shard_map.132.local = f32[256,2048]{1,0:T(8,128)} custom-call(bf16[256,2048]{1,0:T(8,128)(2,1)S(1)} %bitcast.35, bf16[256,128]{1,0:T(8,128)(2,1)S(1)} %bitcast.30, bf16[256,128]{1,0:T(8,128)(2,1)S(1)} %bitcast.37, f32[256,128]{1,0:T(8,128)S(1)} %get-tuple-element.16.run, f32[256,128]{1,0:T(8,128)S(1)} %get-tuple-element.17.step), custom_call_target="tpu_custom_call" | custom-call | flops 4294967296 | bytes 4194304 | tf_op jit(solution)/shard_map/pallas_call | solution.py:505
  19.4 3.9 %all-to-all-done.got.refs_1_ = bf16[16,136,128]{2,1,0:T(8,128)(2,1)S(1)} async-done(((bf16[16,136,128]{2,1,0:T(8,128)(2,1)}), bf16[16,136,128]{2,1,0:T(8,128)(2,1)S(1)}, u32[]{:S(2)}, u32[]{:S(2)}) %all-to-all-start) | async-done | bytes 557088 | tf_op jit(solution)/shard_map/all_to_all | solution.py:451
  23.3 0.1 shard_map.134
  23.4 14.8 %all_to_all.30.got.asked = bf16[16,136,128]{2,1,0:T(8,128)(2,1)S(1)} all-to-all(bf16[16,136,128]{2,1,0:T(8,128)(2,1)S(1)} %shard_map.134), channel_id=1, replica_groups=mesh['dp'=8,'seq_0'=4,'seq_1'=4] {'seq_0','seq_1'}, dimensions={0} | all-to-all | bytes 1114112 | tf_op jit(solution)/shard_map/all_to_all | solution.py:451
  38.2 1.8 %shard_map.135 = (bf16[256,2048]{1,0:T(8,128)(2,1)S(1)}, bf16[16,128,256]{2,1,0:T(8,128)(2,1)S(1)}) custom-call(f32[256,2048]{1,0:T(8,128)S(1)} %copy-done, bf16[16,136,128]{2,1,0:T(8,128)(2,1)S(1)} %all_to_all.30.got.asked, bf16[256,128]{1,0:T(8,128)(2,1)S(1)} %bitcast.38, f32[256,128]{1,0:T(8,128)S(1)} %get-tuple-element.16.run, ...), custom_call_target="tpu_custom_call" | custom-call | flops 2147483648 | bytes 4194304 | tf_op jit(solution)/shard_map/pallas_call | solution.py:517
  40.1 0.0 copy-start.4
  40.1 18.1 %all_to_all.31 = bf16[16,128,256]{2,1,0:T(8,128)(2,1)S(1)} all-to-all(bf16[16,128,256]{2,1,0:T(8,128)(2,1)S(1)} %get-tuple-element.20), channel_id=1, replica_groups=mesh['dp'=8,'seq_0'=4,'seq_1'=4] {'seq_0','seq_1'}, dimensions={0} | all-to-all | bytes 2097152 | tf_op jit(solution)/shard_map/all_to_all | solution.py:451
  58.2 3.1 %shard_map.136 = bf16[2048,256]{1,0:T(8,128)(2,1)S(1)} custom-call(bf16[2048,256]{1,0:T(8,128)(2,1)S(1)} %bitcast.26, f32[1024,128]{1,0:T(8,128)S(1)} %copy-done.10, f32[8,1024]{1,0:T(8,128)S(1)} %copy-done.12, f32[64,16]{1,0:T(8,128)S(1)} %copy-done.13, f32[64,256]{1,0:T(8,128)S(1)} %copy-done.11, f32[64,192]{1,0:T(8,128)S(1)} %bitcast.36), custom_call_target="tpu_custom_call" | custom-call | flops 4294967296 | bytes 4194304 | tf_op jit(solution)/shard_map/pallas_call | solution.py:525
  61.4 16.9 %all_to_all.32 = bf16[16,128,256]{2,1,0:T(8,128)(2,1)S(1)} all-to-all(bf16[16,128,256]{2,1,0:T(8,128)(2,1)S(1)} %bitcast.28), channel_id=1, replica_groups=mesh['dp'=8,'seq_0'=4,'seq_1'=4] {'seq_0','seq_1'}, dimensions={0} | all-to-all | bytes 2097152 | tf_op jit(solution)/shard_map/all_to_all | solution.py:451
  78.3 2.9 %shard_map.137 = (bf16[256,2048]{1,0:T(8,128)(2,1)S(1)}, bf16[16,384,128]{2,1,0:T(8,128)(2,1)S(1)}) custom-call(bf16[2048,256]{1,0:T(8,128)(2,1)S(1)} %bitcast.27, bf16[16,136,128]{2,1,0:T(8,128)(2,1)S(1)} %all_to_all.30.got.asked, bf16[2048,256]{1,0:T(8,128)(2,1)S(1)} %copy-done.3, bf16[256,2048]{1,0:T(8,128)(2,1)S(1)} %get-tuple-element.25.scan_out, ...), custom_call_target="tpu_custom_call" | custom-call | flops 2147483648 | bytes 4194304 | tf_op jit(solution)/shard_map/pallas_call | solution.py:546
  81.2 21.4 %all_to_all.33.got.refs_0_ = bf16[16,384,128]{2,1,0:T(8,128)(2,1)S(1)} all-to-all(bf16[16,384,128]{2,1,0:T(8,128)(2,1)S(1)} %get-tuple-element.27), channel_id=1, replica_groups=mesh['dp'=8,'seq_0'=4,'seq_1'=4] {'seq_0','seq_1'}, dimensions={0} | all-to-all | bytes 3145728 | tf_op jit(solution)/shard_map/all_to_all | solution.py:451
  102.6 0.1 shard_map.139
  102.8 0.1 collective-permute-start
  102.8 1.2 collective-permute-done
  104.1 1.7 %collective-permute-start.1 = (f32[128,128]{1,0:T(8,128)S(1)}, f32[128,128]{1,0:T(8,128)S(1)}, u32[]{:S(2)}, u32[]{:S(2)}) collective-permute-start(f32[128,128]{1,0:T(8,128)S(1)} %add.14), channel_id=1, source_target_pairs={{0,32},{16,48},{32,0},{48,16},{64,96},{80,112},{96,64},{112,80},{1... | collective-permute-start | bytes 196616 | tf_op jit(solution)/shard_map/ppermute | solution.py:475
  105.8 2.7 %collective-permute-done.1 = f32[128,128]{1,0:T(8,128)S(1)} collective-permute-done((f32[128,128]{1,0:T(8,128)S(1)}, f32[128,128]{1,0:T(8,128)S(1)}, u32[]{:S(2)}, u32[]{:S(2)}) %collective-permute-start.1) | collective-permute-done | bytes 65568 | tf_op jit(solution)/shard_map/ppermute | solution.py:475
  108.5 3.2 %collective-permute-start.2 = (f32[128,128]{1,0:T(8,128)S(1)}, f32[128,128]{1,0:T(8,128)S(1)}, u32[]{:S(2)}, u32[]{:S(2)}) collective-permute-start(f32[128,128]{1,0:T(8,128)S(1)} %add.15), channel_id=1, source_target_pairs={{0,64},{16,80},{32,96},{48,112},{64,0},{80,16},{96,32},{112,48},{1... | collective-permute-start | bytes 196616 | tf_op jit(solution)/shard_map/ppermute | solution.py:475
  111.7 3.1 %shard_map.138.refs_3_.within = f32[256,2048]{1,0:T(8,128)S(1)} custom-call(bf16[256,2048]{1,0:T(8,128)(2,1)S(1)} %get-tuple-element.26.og, bf16[256,128]{1,0:T(8,128)(2,1)S(1)} %bitcast.31, bf16[256,128]{1,0:T(8,128)(2,1)S(1)} %bitcast.40, f32[256,128]{1,0:T(8,128)S(1)} %get-tuple-element.16.run), custom_call_target="tpu_custom_call" | custom-call | flops 4294967296 | bytes 4194304 | tf_op jit(solution)/shard_map/pallas_call | solution.py:555
  114.8 0.0 collective-permute-done.2
  114.8 0.2 shard_map.140
  115.1 19.3 %all_to_all.34.got.own = bf16[16,256,128]{2,1,0:T(8,128)(2,1)S(1)} all-to-all(bf16[16,256,128]{2,1,0:T(8,128)(2,1)S(1)} %shard_map.140), channel_id=1, replica_groups=mesh['dp'=8,'seq_0'=4,'seq_1'=4] {'seq_0','seq_1'}, dimensions={0} | all-to-all | bytes 2097152 | tf_op jit(solution)/shard_map/all_to_all | solution.py:451
  134.4 0.1 collective-permute-start.3
  134.5 2.0 %shard_map.141 = bf16[256,2048]{1,0:T(8,128)(2,1)} custom-call(f32[256,2048]{1,0:T(8,128)S(1)} %shard_map.138.refs_3_.within, bf16[16,256,128]{2,1,0:T(8,128)(2,1)S(1)} %all_to_all.34.got.own, bf16[256,128]{1,0:T(8,128)(2,1)S(1)} %bitcast.32, f32[256,128]{1,0:T(8,128)S(1)} %get-tuple-element.16.run, f32[256,128]{1,0:T(8,128)S(1)} %get-tuple-element.17.step), custom_call_target="tpu_custom_call" | custom-call | flops 1073741824 | bytes 4194304 | tf_op jit(solution)/shard_map/pallas_call | solution.py:581
  136.4 0.0 collective-permute-done.3.other
  136.4 1.5 %shard_map.142 = f32[2048,256]{1,0:T(8,128)} custom-call(s32[1]{0:T(128)} %bitcast.3.core, bf16[16,256,128]{2,1,0:T(8,128)(2,1)S(1)} %all_to_all.34.got.own, bf16[16,128,128]{2,1,0:T(8,128)(2,1)S(1)} %collective-permute-done.3.other), custom_call_target="tpu_custom_call" | custom-call | bytes 4194304 | tf_op jit(solution)/shard_map/pallas_call | solution.py:584
  (30 shorter events, 0.1 us)
Async XLA Ops:
  0.6 11.1 %copy-start.14 = (f32[1,8,3]{1,0,2:T(1,128)S(1)}, f32[1,8,3]{1,0,2:T(1,128)}, u32[]{:S(2)}) copy-start(f32[1,8,3]{1,0,2:T(1,128)} %param.22) | copy-start | bytes 292
  0.6 11.1 %copy-start.9 = (s32[1,64]{1,0:T(1,128)S(1)}, s32[1,64]{1,0:T(1,128)}, u32[]{:S(2)}) copy-start(s32[1,64]{1,0:T(1,128)} %camera.1) | copy-start | bytes 772
  0.7 11.1 %copy-start.7 = (s32[1,64,16]{1,2,0:T(8,128)S(1)}, s32[1,64,16]{1,2,0:T(8,128)}, u32[]{:S(2)}) copy-start(s32[1,64,16]{1,2,0:T(8,128)} %param.20) | copy-start | bytes 12292
  0.7 11.1 %copy-start.8 = (s32[1,64]{1,0:T(1,128)S(1)}, s32[1,64]{1,0:T(1,128)}, u32[]{:S(2)}) copy-start(s32[1,64]{1,0:T(1,128)} %count.1) | copy-start | bytes 772
  0.7 11.1 %copy-start.6 = (s32[1,64,16]{1,2,0:T(8,128)S(1)}, s32[1,64,16]{1,2,0:T(8,128)}, u32[]{:S(2)}) copy-start(s32[1,64,16]{1,2,0:T(8,128)} %param.18) | copy-start | bytes 12292
  3.7 19.5 %all-to-all-start = ((bf16[16,136,128]{2,1,0:T(8,128)(2,1)}), bf16[16,136,128]{2,1,0:T(8,128)(2,1)S(1)}, u32[]{:S(2)}, u32[]{:S(2)}) async-start(bf16[16,136,128]{2,1,0:T(8,128)(2,1)} %get-tuple-element.18), calls=%async_computation | async-start | bytes 1114112 | tf_op jit(solution)/shard_map/all_to_all | solution.py:451
  11.8 2.0 %copy-start.1 = (bf16[1,256,128]{2,1,0:T(8,128)(2,1)S(1)}, bf16[1,256,128]{2,1,0:T(8,128)(2,1)}, u32[]{:S(2)}) copy-start(bf16[1,256,128]{2,1,0:T(8,128)(2,1)} %param.13) | copy-start | bytes 196612
  11.8 2.0 %copy-start.2 = (bf16[1,256,2048]{2,1,0:T(8,128)(2,1)S(1)}, bf16[1,256,2048]{2,1,0:T(8,128)(2,1)}, u32[]{:S(2)}) copy-start(bf16[1,256,2048]{2,1,0:T(8,128)(2,1)} %param.12) | copy-start | bytes 3145732
  11.8 2.0 %copy-start.5 = (bf16[1,256,128]{2,1,0:T(8,128)(2,1)S(1)}, bf16[1,256,128]{2,1,0:T(8,128)(2,1)}, u32[]{:S(2)}) copy-start(bf16[1,256,128]{2,1,0:T(8,128)(2,1)} %param.14) | copy-start | bytes 196612
  23.3 15.0 %copy-start = (f32[256,2048]{1,0:T(8,128)S(1)}, f32[256,2048]{1,0:T(8,128)}, u32[]{:S(2)}) copy-start(f32[256,2048]{1,0:T(8,128)} %shard_map.132.local) | copy-start | bytes 6291460
  23.3 15.0 %copy-start.3 = (bf16[2048,256]{1,0:T(8,128)(2,1)S(1)}, bf16[2048,256]{1,0:T(8,128)(2,1)}, u32[]{:S(2)}) copy-start(bf16[2048,256]{1,0:T(8,128)(2,1)} %weight.3) | copy-start | bytes 3145732
  40.1 18.2 %copy-start.4 = (f32[1,64,192]{2,1,0:T(8,128)S(1)}, f32[1,64,192]{2,1,0:T(8,128)}, u32[]{:S(2)}) copy-start(f32[1,64,192]{2,1,0:T(8,128)} %param.23) | copy-start | bytes 147460
  40.1 18.1 %copy-start.10 = (f32[1024,128]{1,0:T(8,128)S(1)}, f32[1024,128]{1,0:T(8,128)}, u32[]{:S(2)}) copy-start(f32[1024,128]{1,0:T(8,128)} %get-tuple-element.21.place_col) | copy-start | bytes 1572868
  40.1 18.1 %copy-start.11 = (f32[64,256]{1,0:T(8,128)S(1)}, f32[64,256]{1,0:T(8,128)}, u32[]{:S(2)}) copy-start(f32[64,256]{1,0:T(8,128)} %get-tuple-element.24.tile_gain) | copy-start | bytes 196612
  40.1 18.1 %copy-start.12 = (f32[8,1024]{1,0:T(8,128)S(1)}, f32[8,1024]{1,0:T(8,128)}, u32[]{:S(2)}) copy-start(f32[8,1024]{1,0:T(8,128)} %get-tuple-element.22.place_row) | copy-start | bytes 98308
  40.1 18.1 %copy-start.13 = (f32[64,16]{1,0:T(8,128)S(1)}, f32[64,16]{1,0:T(8,128)}, u32[]{:S(2)}) copy-start(f32[64,16]{1,0:T(8,128)} %get-tuple-element.23.live) | copy-start | bytes 12292
  102.8 1.3 collective-permute-start
  104.1 4.3 %collective-permute-start.1 = (f32[128,128]{1,0:T(8,128)S(1)}, f32[128,128]{1,0:T(8,128)S(1)}, u32[]{:S(2)}, u32[]{:S(2)}) collective-permute-start(f32[128,128]{1,0:T(8,128)S(1)} %add.14), channel_id=1, source_target_pairs={{0,32},{16,48},{32,0},{48,16},{64,96},{80,112},{96,64},{112,80},{1... | collective-permute-start | bytes 196616 | tf_op jit(solution)/shard_map/ppermute | solution.py:475
  108.5 6.4 %collective-permute-start.2 = (f32[128,128]{1,0:T(8,128)S(1)}, f32[128,128]{1,0:T(8,128)S(1)}, u32[]{:S(2)}, u32[]{:S(2)}) collective-permute-start(f32[128,128]{1,0:T(8,128)S(1)} %add.15), channel_id=1, source_target_pairs={{0,64},{16,80},{32,96},{48,112},{64,0},{80,16},{96,32},{112,48},{1... | collective-permute-start | bytes 196616 | tf_op jit(solution)/shard_map/ppermute | solution.py:475
  134.4 2.1 %collective-permute-start.3 = (bf16[16,128,128]{2,1,0:T(8,128)(2,1)S(1)}, bf16[16,128,128]{2,1,0:T(8,128)(2,1)S(1)}, u32[]{:S(2)}, u32[]{:S(2)}) collective-permute-start(bf16[16,128,128]{2,1,0:T(8,128)(2,1)S(1)} %slice.4), channel_id=1, source_target_pairs={{0,16},{16,0},{32,48},{48,32},{64,80},{80,64},{96,112},{112,96},{1... | collective-permute-start | bytes 1572872 | tf_op jit(solution)/shard_map/ppermute | solution.py:475

commit v3 on v2

--- a/solution.py
+++ b/solution.py
@@ -315,12 +315,13 @@
 def composite_body(
     ans, place_col, place_row, live, tile_gain, target, out, slots, keep, trans, grads
 ):
-    lane_f = iota((256, 128), 1).astype(F32)
+    one, zero = jnp.ones((256, 128), BF16), jnp.zeros((256, 128), BF16)
+    lane_o = iota((256, 128), 1).astype(jnp.int16)
     for b in range(ROWS // 256):
         rows = slice(b * 256, (b + 1) * 256)
-        place = place_col[rows, :]
+        place = place_col[rows, :].astype(jnp.int32).astype(jnp.int16)
         hot = jnp.concatenate(
-            [(place == lane_f + 128.0 * o).astype(F32).astype(BF16) for o in range(OWN)], axis=1
+            [jnp.where(place == lane_o + np.int16(128 * o), one, zero) for o in range(OWN)], axis=1
         )
         slots[rows, :] = dot(hot, ans[...])
     lane = iota((TILES, 128), 1)
@@ -379,7 +380,7 @@
 HALF = 128
 
 
-def token_grad_body(homed, asked, weight, scan_out, rd, run, out_grad, pay):
+def token_grad_body(core, homed, asked, scan_out, low_out, mine, theirs):
     token = iota((TOK, 128), 0).astype(F32)
     hot = jnp.concatenate(
         [
@@ -388,31 +389,44 @@
         ],
         axis=1,
     )
-    feat = dot(hot, homed[...])
-    low = feat.astype(BF16)
+    low = dot(hot, homed[...]).astype(BF16)
+    low_out[...] = low
     low_t = turned(low)
+    first = core[0] == 0
+    upper, lower = low_t[0:HALF, :].astype(F32), low_t[HALF:FEAT, :].astype(F32)
+    own = jnp.where(first, upper, lower).astype(BF16)
+    far = jnp.where(first, lower, upper).astype(BF16)
+    for c in range(NCH):
+        for rows, out in ((far, theirs), (own, mine)):
+            piece = dot(rows, scan_out[:, cols(c)]).astype(BF16)
+            for k in range(2):
+                out[2 * c + k] = piece[:, k * 128 : (k + 1) * 128]
+
+
+def out_grad_body(low, weight, rd, run, out_grad, ends):
     base = spreader()
     lead = split_pair(jnp.exp(run[...]))
     rt = turned(rd[...])
     for c in range(NCH):
-        og = dot_t(low, weight[cols(c), :]).astype(BF16)
+        og = dot_t(low[...], weight[cols(c), :]).astype(BF16)
         out_grad[:, cols(c)] = og
         scaled = (og.astype(F32) * dot(lead, spread_of(base, c))).astype(BF16)
         end = dot(rt, scaled).astype(BF16)
-        part = dot(low_t, scan_out[:, cols(c)]).astype(BF16)
         for k in range(2):
-            lanes = slice(k * 128, (k + 1) * 128)
-            pay[2 * c + k, 0:NST, :] = end[:, lanes]
-            pay[2 * c + k, NST : NST + FEAT, :] = part[:, lanes]
-
-
-def scene_sum_body(core, got, mine, theirs):
-    total = jnp.zeros((FEAT, 128), F32)
+            ends[2 * c + k] = end[:, k * 128 : (k + 1) * 128]
+
+
+def join_body(ends, mine, other, pay):
+    for g in range(OWN):
+        pay[g, 0:NST, :] = ends[g]
+        pay[g, NST : NST + HALF, :] = (mine[g].astype(F32) + other[g].astype(F32)).astype(BF16)
+
+
+def scene_sum_body(got, part):
+    total = jnp.zeros((HALF, 128), F32)
     for d in range(OWN):
-        total = total + got[d, NST : NST + FEAT, :].astype(F32)
-    first = core[0] == 0
-    mine[...] = jnp.where(first, total[0:HALF, :], total[HALF:FEAT, :])
-    theirs[...] = jnp.where(first, total[HALF:FEAT, :], total[0:HALF, :])
+        total = total + got[d, NST : NST + HALF, :].astype(F32)
+    part[...] = total
 
 
 def suffix_body(scale, got, tails, part, within, pay):
@@ -543,14 +557,25 @@
         target_color[0],
     )
     homed = swap(outgoing.reshape(OWN, 128, FEAT), SEQ)
-    out_grad, pay = call(
+    low, mine, theirs = call(
         token_grad_body,
-        [((TOK, WID), BF16, 1), ((OWN, NST + FEAT, 128), BF16)],
-        [VMEM, TAIL_SPEC, VMEM, VMEM, VMEM, VMEM],
-        [VMEM, VMEM],
+        [((TOK, FEAT), BF16, 1), ((OWN, HALF, 128), BF16), ((OWN, HALF, 128), BF16)],
+        [SMEM, VMEM, TAIL_SPEC, VMEM],
+        [VMEM] * 3,
         grid=(1,),
         flops=1 << 31,
-    )(homed.reshape(OWN * 128, FEAT), states, head_weight, held(scan_out), rd, held(run))
+    )(core_ref, homed.reshape(OWN * 128, FEAT), states, held(scan_out))
+    other = trade(theirs, 1)
+    out_grad, back_ends = call(
+        out_grad_body,
+        [((TOK, WID), BF16, 1), ((OWN, NST, 128), BF16, 1)],
+        [VMEM] * 4,
+        [VMEM, VMEM],
+        flops=1 << 31,
+    )(held(low), head_weight, rd, held(run))
+    (pay,) = call(
+        join_body, [((OWN, NST + HALF, 128), BF16)], [VMEM] * 3, [VMEM]
+    )(held(back_ends), mine, other)
     back = swap(pay, SEQ)
     (within,) = call(
         back_local_body,
@@ -560,14 +585,8 @@
         scratch=[buf((NST, WID), BF16)],
         flops=1 << 32,
     )(held(out_grad), wr, rd, held(run))
-    mine, theirs = call(
-        scene_sum_body, [((HALF, 128), F32)] * 2, [SMEM, VMEM], [VMEM] * 2
-    )(core_ref, back)
-    part = mine + trade(theirs, 1)
-    hop = 2
-    while hop < scenes:
-        part = part + trade(part, hop)
-        hop *= 2
+    (part,) = call(scene_sum_body, [((HALF, 128), F32)], [VMEM], [VMEM])(back)
+    part = (part + trade(part, 2)) + (trade(part, 4) + trade(part, 6))
     scale = np.float32(1.0 / np.sqrt(float(scenes * TOK * lax.axis_size(SEQ))))
     (pay,) = call(
         lambda *refs: suffix_body(scale, *refs),

time: 140 us -> 136 us (0.971)
  waiting for transfers between devices: 7.8 us -> 5.41 us
    ppermute x4 -> x5, waiting for transfers between devices: 3.91 us -> 1.51 us  [trade(): return lax.ppermute(v, 'dp', [(i, i ^ hop) for i in range(scenes)])]
    ppermute x4 -> x5, starting transfers between devices: 5.09 us -> 4.34 us  [trade(): return lax.ppermute(v, 'dp', [(i, i ^ hop) for i in range(scenes)])]
    pallas_call x2 -> x4, Pallas kernels: 3.08 us -> 3.52 us  [the longest x1 1.93 us: shards(): call(out_grad_body, [((TOK, WID), BF16, 1), ((OWN, NST, 128), BF16, 1)],...]
  transfers between devices with their start and end apart: 5 -> 6, of which waited for: 3 -> 2; matrix products, arithmetic and copies ran while one was open for 0% -> 0% of each run, Pallas kernels for 9% -> 11%
where the time goes in v3:
time: 136 us; the launch traced here: 134 us
  blocking collectives  89.4 us (66%)
  Pallas kernels  25.9 us (19%)
  starting transfers between devices  12.3 us (9%)
  waiting for transfers between devices  5.41 us (4%)
    all_to_all x5, blocking collectives, swap(): return lax.all_to_all(x, axes, split_axis=0, concat_axis=0, tiled=True)  89.4 us
    all_to_all x1, starting transfers between devices, swap(): return lax.all_to_all(x, axes, split_axis=0, concat_axis=0, tiled=True)  7.97 us
    pallas_call x1, Pallas kernels, shards(): call(fore_local_body, [((TOK, WID), F32, 0)], [VMEM] * 5, [VMEM], scratch...  5.59 us
    ppermute x5, starting transfers between devices, trade(): return lax.ppermute(v, 'dp', [(i, i ^ hop) for i in range(scenes)])  4.34 us
    all_to_all x1, waiting for transfers between devices, swap(): return lax.all_to_all(x, axes, split_axis=0, concat_axis=0, tiled=True)  3.9 us
    pallas_call x1, Pallas kernels, shards(): call(back_local_body, [((TOK, WID), F32, 1)], [VMEM] * 4, [VMEM], scratch...  3.12 us
    pallas_call x1, Pallas kernels, shards(): call(composite_body, [((OWN * 128, FEAT), BF16)], [VMEM] * 6, [VMEM], scr...  3.1 us
    pallas_call x1, Pallas kernels, shards(): call(local_end_body, [((OWN, NST + TAIL, 128), BF16), ((TOK, 128), F32, 1...  3.03 us
  transfers between devices with their start and end apart: 6, of which 2 were waited for; matrix products, arithmetic and copies ran while one was open for 0% of the time, Pallas kernels for 11%

profile of v3, /device:TPU:0, one launch (start us, length us, event | category | flops | bytes accessed | tf_op | source)
XLA Modules:
  0.0 134.0 jit_solution(17411719777730131324)
XLA Ops:
  0.7 3.0 %shard_map.131 = (bf16[16,136,128]{2,1,0:T(8,128)(2,1)}, f32[256,128]{1,0:T(8,128)S(1)}, f32[256,128]{1,0:T(8,128)S(1)}) custom-call(s32[1]{0:T(128)} %bitcast.core, bf16[256,2048]{1,0:T(8,128)(2,1)} %bitcast.34, bf16[256,128]{1,0:T(8,128)(2,1)} %bitcast.29, f32[64,256]{1,0:T(8,128)} %bitcast.44, f32[64,256]{1,0:T(8,128)} %bitcast.45), custom_call_target="tpu_custom_call" | custom-call | flops 536870912 | bytes 4194304 | tf_op jit(solution)/shard_map/pallas_call | solution.py:491
  3.7 8.0 %all-to-all-start = ((bf16[16,136,128]{2,1,0:T(8,128)(2,1)}), bf16[16,136,128]{2,1,0:T(8,128)(2,1)S(1)}, u32[]{:S(2)}, u32[]{:S(2)}) async-start(bf16[16,136,128]{2,1,0:T(8,128)(2,1)} %get-tuple-element.19), calls=%async_computation | async-start | bytes 1114112 | tf_op jit(solution)/shard_map/all_to_all | solution.py:465
  11.8 0.0 copy-start.1
  11.8 0.0 copy-start.2
  11.8 0.0 copy-start.5
  11.8 1.9 %shard_map.133 = (bf16[16,8,128]{2,1,0:T(8,128)(2,1)S(1)}, f32[1024,128]{1,0:T(8,128)}, f32[8,1024]{1,0:T(8,128)}, f32[64,16]{1,0:T(8,128)}, f32[64,256]{1,0:T(8,128)}) custom-call(s32[16,64]{1,0:T(8,128)S(1)} %bitcast.41, s32[16,64]{1,0:T(8,128)S(1)} %bitcast.42, s32[1,64]{1,0:T(1,128)S(1)} %copy-done.8, s32[1,64]{1,0:T(1,128)S(1)} %copy-done.9, ...), custom_call_target="tpu_custom_call" | custom-call | flops 2147483648 | bytes 4194304 | tf_op jit(solution)/shard_map/pallas_call | solution.py:506
  13.8 5.6 %shard_map.132.local = f32[256,2048]{1,0:T(8,128)} custom-call(bf16[256,2048]{1,0:T(8,128)(2,1)S(1)} %bitcast.35, bf16[256,128]{1,0:T(8,128)(2,1)S(1)} %bitcast.30, bf16[256,128]{1,0:T(8,128)(2,1)S(1)} %bitcast.37, f32[256,128]{1,0:T(8,128)S(1)} %get-tuple-element.17.run, f32[256,128]{1,0:T(8,128)S(1)} %get-tuple-element.18.step), custom_call_target="tpu_custom_call" | custom-call | flops 4294967296 | bytes 4194304 | tf_op jit(solution)/shard_map/pallas_call | solution.py:519
  19.4 3.9 %all-to-all-done.got.refs_1_ = bf16[16,136,128]{2,1,0:T(8,128)(2,1)S(1)} async-done(((bf16[16,136,128]{2,1,0:T(8,128)(2,1)}), bf16[16,136,128]{2,1,0:T(8,128)(2,1)S(1)}, u32[]{:S(2)}, u32[]{:S(2)}) %all-to-all-start) | async-done | bytes 557088 | tf_op jit(solution)/shard_map/all_to_all | solution.py:465
  23.3 0.1 shard_map.134
  23.4 14.8 %all_to_all.30.got.asked = bf16[16,136,128]{2,1,0:T(8,128)(2,1)S(1)} all-to-all(bf16[16,136,128]{2,1,0:T(8,128)(2,1)S(1)} %shard_map.134), channel_id=1, replica_groups=mesh['dp'=8,'seq_0'=4,'seq_1'=4] {'seq_0','seq_1'}, dimensions={0} | all-to-all | bytes 1114112 | tf_op jit(solution)/shard_map/all_to_all | solution.py:465
  38.2 1.8 %shard_map.135 = (bf16[256,2048]{1,0:T(8,128)(2,1)S(1)}, bf16[16,128,256]{2,1,0:T(8,128)(2,1)S(1)}) custom-call(f32[256,2048]{1,0:T(8,128)S(1)} %copy-done, bf16[16,136,128]{2,1,0:T(8,128)(2,1)S(1)} %all_to_all.30.got.asked, bf16[256,128]{1,0:T(8,128)(2,1)S(1)} %bitcast.38, f32[256,128]{1,0:T(8,128)S(1)} %get-tuple-element.17.run, ...), custom_call_target="tpu_custom_call" | custom-call | flops 2147483648 | bytes 4194304 | tf_op jit(solution)/shard_map/pallas_call | solution.py:531
  40.0 0.0 copy-start.4
  40.1 18.1 %all_to_all.31 = bf16[16,128,256]{2,1,0:T(8,128)(2,1)S(1)} all-to-all(bf16[16,128,256]{2,1,0:T(8,128)(2,1)S(1)} %get-tuple-element.21), channel_id=1, replica_groups=mesh['dp'=8,'seq_0'=4,'seq_1'=4] {'seq_0','seq_1'}, dimensions={0} | all-to-all | bytes 2097152 | tf_op jit(solution)/shard_map/all_to_all | solution.py:465
  58.2 3.1 %shard_map.136 = bf16[2048,256]{1,0:T(8,128)(2,1)S(1)} custom-call(bf16[2048,256]{1,0:T(8,128)(2,1)S(1)} %bitcast.27, f32[1024,128]{1,0:T(8,128)S(1)} %copy-done.10, f32[8,1024]{1,0:T(8,128)S(1)} %copy-done.12, f32[64,16]{1,0:T(8,128)S(1)} %copy-done.13, f32[64,256]{1,0:T(8,128)S(1)} %copy-done.11, f32[64,192]{1,0:T(8,128)S(1)} %bitcast.36), custom_call_target="tpu_custom_call" | custom-call | flops 4294967296 | bytes 4194304 | tf_op jit(solution)/shard_map/pallas_call | solution.py:539
  61.3 16.9 %all_to_all.32 = bf16[16,128,256]{2,1,0:T(8,128)(2,1)S(1)} all-to-all(bf16[16,128,256]{2,1,0:T(8,128)(2,1)S(1)} %bitcast.28), channel_id=1, replica_groups=mesh['dp'=8,'seq_0'=4,'seq_1'=4] {'seq_0','seq_1'}, dimensions={0} | all-to-all | bytes 2097152 | tf_op jit(solution)/shard_map/all_to_all | solution.py:465
  78.3 1.4 %shard_map.137 = (bf16[256,256]{1,0:T(8,128)(2,1)S(1)}, bf16[16,128,128]{2,1,0:T(8,128)(2,1)S(1)}, bf16[16,128,128]{2,1,0:T(8,128)(2,1)S(1)}) custom-call(s32[1]{0:T(128)} %bitcast.core, bf16[2048,256]{1,0:T(8,128)(2,1)S(1)} %bitcast.26, bf16[16,136,128]{2,1,0:T(8,128)(2,1)S(1)} %all_to_all.30.got.asked, bf16[256,2048]{1,0:T(8,128)(2,1)S(1)} %get-tuple-element.26.scan_out), custom_call_target="tpu_custom_call" | custom-call | flops 2147483648 | bytes 4194304 | tf_op jit(solution)/shard_map/pallas_call | solution.py:560
  79.7 0.1 collective-permute-start
  79.8 1.9 %shard_map.138 = (bf16[256,2048]{1,0:T(8,128)(2,1)S(1)}, bf16[16,128,128]{2,1,0:T(8,128)(2,1)S(1)}) custom-call(bf16[256,256]{1,0:T(8,128)(2,1)S(1)} %get-tuple-element.27.low, bf16[2048,256]{1,0:T(8,128)(2,1)S(1)} %copy-done.3, bf16[256,128]{1,0:T(8,128)(2,1)S(1)} %bitcast.39, f32[256,128]{1,0:T(8,128)S(1)} %get-tuple-element.17.run), custom_call_target="tpu_custom_call" | custom-call | flops 2147483648 | bytes 4194304 | tf_op jit(solution)/shard_map/pallas_call | solution.py:569
  81.7 0.0 collective-permute-done.other
  81.7 0.1 shard_map.140
  81.8 21.0 %all_to_all.33.got.refs_0_ = bf16[16,256,128]{2,1,0:T(8,128)(2,1)S(1)} all-to-all(bf16[16,256,128]{2,1,0:T(8,128)(2,1)S(1)} %shard_map.140), channel_id=1, replica_groups=mesh['dp'=8,'seq_0'=4,'seq_1'=4] {'seq_0','seq_1'}, dimensions={0} | all-to-all | bytes 2097152 | tf_op jit(solution)/shard_map/all_to_all | solution.py:465
  102.9 0.1 shard_map.141
  102.9 3.0 %collective-permute-start.3 = (f32[128,128]{1,0:T(8,128)S(1)}, f32[128,128]{1,0:T(8,128)S(1)}, u32[]{:S(2)}, u32[]{:S(2)}) collective-permute-start(f32[128,128]{1,0:T(8,128)S(1)} %shard_map.141), channel_id=1, source_target_pairs={{0,96},{16,112},{32,64},{48,80},{64,32},{80,48},{96,0},{112,16},{1... | collective-permute-start | bytes 196616 | tf_op jit(solution)/shard_map/ppermute | solution.py:489
  106.0 0.7 collective-permute-start.2
  106.7 0.4 collective-permute-start.1
  107.1 3.1 %shard_map.139.refs_3_.within = f32[256,2048]{1,0:T(8,128)S(1)} custom-call(bf16[256,2048]{1,0:T(8,128)(2,1)S(1)} %get-tuple-element.28.og, bf16[256,128]{1,0:T(8,128)(2,1)S(1)} %bitcast.31, bf16[256,128]{1,0:T(8,128)(2,1)S(1)} %bitcast.40, f32[256,128]{1,0:T(8,128)S(1)} %get-tuple-element.17.run), custom_call_target="tpu_custom_call" | custom-call | flops 4294967296 | bytes 4194304 | tf_op jit(solution)/shard_map/pallas_call | solution.py:580
  110.2 1.5 %collective-permute-done.2 = f32[128,128]{1,0:T(8,128)S(1)} collective-permute-done((f32[128,128]{1,0:T(8,128)S(1)}, f32[128,128]{1,0:T(8,128)S(1)}, u32[]{:S(2)}, u32[]{:S(2)}) %collective-permute-start.2) | collective-permute-done | bytes 65568 | tf_op jit(solution)/shard_map/ppermute | solution.py:489
  111.8 0.2 shard_map.142
  112.0 18.5 %all_to_all.34.got.own = bf16[16,256,128]{2,1,0:T(8,128)(2,1)S(1)} all-to-all(bf16[16,256,128]{2,1,0:T(8,128)(2,1)S(1)} %shard_map.142), channel_id=1, replica_groups=mesh['dp'=8,'seq_0'=4,'seq_1'=4] {'seq_0','seq_1'}, dimensions={0} | all-to-all | bytes 2097152 | tf_op jit(solution)/shard_map/all_to_all | solution.py:465
  130.5 0.1 collective-permute-start.4
  130.6 2.0 %shard_map.143 = bf16[256,2048]{1,0:T(8,128)(2,1)} custom-call(f32[256,2048]{1,0:T(8,128)S(1)} %shard_map.139.refs_3_.within, bf16[16,256,128]{2,1,0:T(8,128)(2,1)S(1)} %all_to_all.34.got.own, bf16[256,128]{1,0:T(8,128)(2,1)S(1)} %bitcast.32, f32[256,128]{1,0:T(8,128)S(1)} %get-tuple-element.17.run, f32[256,128]{1,0:T(8,128)S(1)} %get-tuple-element.18.step), custom_call_target="tpu_custom_call" | custom-call | flops 1073741824 | bytes 4194304 | tf_op jit(solution)/shard_map/pallas_call | solution.py:600
  132.6 1.5 %shard_map.144 = f32[2048,256]{1,0:T(8,128)} custom-call(s32[1]{0:T(128)} %bitcast.core, bf16[16,256,128]{2,1,0:T(8,128)(2,1)S(1)} %all_to_all.34.got.own, bf16[16,128,128]{2,1,0:T(8,128)(2,1)S(1)} %collective-permute-done.4.other), custom_call_target="tpu_custom_call" | custom-call | bytes 4194304 | tf_op jit(solution)/shard_map/pallas_call | solution.py:603
  (32 shorter events, 0.1 us)
Async XLA Ops:
  0.6 11.1 %copy-start.14 = (f32[1,8,3]{1,0,2:T(1,128)S(1)}, f32[1,8,3]{1,0,2:T(1,128)}, u32[]{:S(2)}) copy-start(f32[1,8,3]{1,0,2:T(1,128)} %param.22) | copy-start | bytes 292
  0.6 11.1 %copy-start.9 = (s32[1,64]{1,0:T(1,128)S(1)}, s32[1,64]{1,0:T(1,128)}, u32[]{:S(2)}) copy-start(s32[1,64]{1,0:T(1,128)} %camera.1) | copy-start | bytes 772
  0.7 11.1 %copy-start.7 = (s32[1,64,16]{1,2,0:T(8,128)S(1)}, s32[1,64,16]{1,2,0:T(8,128)}, u32[]{:S(2)}) copy-start(s32[1,64,16]{1,2,0:T(8,128)} %param.20) | copy-start | bytes 12292
  0.7 11.1 %copy-start.8 = (s32[1,64]{1,0:T(1,128)S(1)}, s32[1,64]{1,0:T(1,128)}, u32[]{:S(2)}) copy-start(s32[1,64]{1,0:T(1,128)} %count.1) | copy-start | bytes 772
  0.7 11.1 %copy-start.6 = (s32[1,64,16]{1,2,0:T(8,128)S(1)}, s32[1,64,16]{1,2,0:T(8,128)}, u32[]{:S(2)}) copy-start(s32[1,64,16]{1,2,0:T(8,128)} %param.18) | copy-start | bytes 12292
  3.7 19.5 %all-to-all-start = ((bf16[16,136,128]{2,1,0:T(8,128)(2,1)}), bf16[16,136,128]{2,1,0:T(8,128)(2,1)S(1)}, u32[]{:S(2)}, u32[]{:S(2)}) async-start(bf16[16,136,128]{2,1,0:T(8,128)(2,1)} %get-tuple-element.19), calls=%async_computation | async-start | bytes 1114112 | tf_op jit(solution)/shard_map/all_to_all | solution.py:465
  11.8 2.0 %copy-start.1 = (bf16[1,256,128]{2,1,0:T(8,128)(2,1)S(1)}, bf16[1,256,128]{2,1,0:T(8,128)(2,1)}, u32[]{:S(2)}) copy-start(bf16[1,256,128]{2,1,0:T(8,128)(2,1)} %param.13) | copy-start | bytes 196612
  11.8 2.0 %copy-start.2 = (bf16[1,256,2048]{2,1,0:T(8,128)(2,1)S(1)}, bf16[1,256,2048]{2,1,0:T(8,128)(2,1)}, u32[]{:S(2)}) copy-start(bf16[1,256,2048]{2,1,0:T(8,128)(2,1)} %param.12) | copy-start | bytes 3145732
  11.8 2.0 %copy-start.5 = (bf16[1,256,128]{2,1,0:T(8,128)(2,1)S(1)}, bf16[1,256,128]{2,1,0:T(8,128)(2,1)}, u32[]{:S(2)}) copy-start(bf16[1,256,128]{2,1,0:T(8,128)(2,1)} %param.14) | copy-start | bytes 196612
  23.3 15.0 %copy-start = (f32[256,2048]{1,0:T(8,128)S(1)}, f32[256,2048]{1,0:T(8,128)}, u32[]{:S(2)}) copy-start(f32[256,2048]{1,0:T(8,128)} %shard_map.132.local) | copy-start | bytes 6291460
  23.3 15.0 %copy-start.3 = (bf16[2048,256]{1,0:T(8,128)(2,1)S(1)}, bf16[2048,256]{1,0:T(8,128)(2,1)}, u32[]{:S(2)}) copy-start(bf16[2048,256]{1,0:T(8,128)(2,1)} %weight.3) | copy-start | bytes 3145732
  40.0 18.2 %copy-start.4 = (f32[1,64,192]{2,1,0:T(8,128)S(1)}, f32[1,64,192]{2,1,0:T(8,128)}, u32[]{:S(2)}) copy-start(f32[1,64,192]{2,1,0:T(8,128)} %param.23) | copy-start | bytes 147460
  40.1 18.1 %copy-start.10 = (f32[1024,128]{1,0:T(8,128)S(1)}, f32[1024,128]{1,0:T(8,128)}, u32[]{:S(2)}) copy-start(f32[1024,128]{1,0:T(8,128)} %get-tuple-element.22.place_col) | copy-start | bytes 1572868
  40.1 18.1 %copy-start.11 = (f32[64,256]{1,0:T(8,128)S(1)}, f32[64,256]{1,0:T(8,128)}, u32[]{:S(2)}) copy-start(f32[64,256]{1,0:T(8,128)} %get-tuple-element.25.tile_gain) | copy-start | bytes 196612
  40.1 18.1 %copy-start.12 = (f32[8,1024]{1,0:T(8,128)S(1)}, f32[8,1024]{1,0:T(8,128)}, u32[]{:S(2)}) copy-start(f32[8,1024]{1,0:T(8,128)} %get-tuple-element.23.place_row) | copy-start | bytes 98308
  40.1 18.1 %copy-start.13 = (f32[64,16]{1,0:T(8,128)S(1)}, f32[64,16]{1,0:T(8,128)}, u32[]{:S(2)}) copy-start(f32[64,16]{1,0:T(8,128)} %get-tuple-element.24.live) | copy-start | bytes 12292
  79.7 2.0 %collective-permute-start = (bf16[16,128,128]{2,1,0:T(8,128)(2,1)S(1)}, bf16[16,128,128]{2,1,0:T(8,128)(2,1)S(1)}, u32[]{:S(2)}, u32[]{:S(2)}) collective-permute-start(bf16[16,128,128]{2,1,0:T(8,128)(2,1)S(1)} %get-tuple-element.31), channel_id=1, source_target_pairs={{0,16},{16,0},{32,48},{48,32},{64,80},{80,64},{96,112},{112,96},{1... | collective-permute-start | bytes 1572872 | tf_op jit(solution)/shard_map/ppermute | solution.py:489
  102.9 7.3 %collective-permute-start.3 = (f32[128,128]{1,0:T(8,128)S(1)}, f32[128,128]{1,0:T(8,128)S(1)}, u32[]{:S(2)}, u32[]{:S(2)}) collective-permute-start(f32[128,128]{1,0:T(8,128)S(1)} %shard_map.141), channel_id=1, source_target_pairs={{0,96},{16,112},{32,64},{48,80},{64,32},{80,48},{96,0},{112,16},{1... | collective-permute-start | bytes 196616 | tf_op jit(solution)/shard_map/ppermute | solution.py:489
  106.0 5.8 %collective-permute-start.2 = (f32[128,128]{1,0:T(8,128)S(1)}, f32[128,128]{1,0:T(8,128)S(1)}, u32[]{:S(2)}, u32[]{:S(2)}) collective-permute-start(f32[128,128]{1,0:T(8,128)S(1)} %shard_map.141), channel_id=1, source_target_pairs={{0,64},{16,80},{32,96},{48,112},{64,0},{80,16},{96,32},{112,48},{1... | collective-permute-start | bytes 196616 | tf_op jit(solution)/shard_map/ppermute | solution.py:489
  106.7 5.1 %collective-permute-start.1 = (f32[128,128]{1,0:T(8,128)S(1)}, f32[128,128]{1,0:T(8,128)S(1)}, u32[]{:S(2)}, u32[]{:S(2)}) collective-permute-start(f32[128,128]{1,0:T(8,128)S(1)} %shard_map.141), channel_id=1, source_target_pairs={{0,32},{16,48},{32,0},{48,16},{64,96},{80,112},{96,64},{112,80},{1... | collective-permute-start | bytes 196616 | tf_op jit(solution)/shard_map/ppermute | solution.py:489
  130.5 2.1 %collective-permute-start.4 = (bf16[16,128,128]{2,1,0:T(8,128)(2,1)S(1)}, bf16[16,128,128]{2,1,0:T(8,128)(2,1)S(1)}, u32[]{:S(2)}, u32[]{:S(2)}) collective-permute-start(bf16[16,128,128]{2,1,0:T(8,128)(2,1)S(1)} %slice.4), channel_id=1, source_target_pairs={{0,16},{16,0},{32,48},{48,32},{64,80},{80,64},{96,112},{112,96},{1... | collective-permute-start | bytes 1572872 | tf_op jit(solution)/shard_map/ppermute | solution.py:489

commit v4 on v3

--- a/solution.py
+++ b/solution.py
@@ -78,7 +78,7 @@
     return pltpu.with_memory_space_constraint(x, pltpu.HBM)
 
 
-def call(body, outs, ins, out_specs, scratch=(), limit=16, flops=0, grid=()):
+def call(body, outs, ins, out_specs, scratch=(), limit=16, flops=0, grid=(), alias=None):
     return pl.pallas_call(
         body,
         out_shape=[
@@ -89,6 +89,7 @@
             grid=grid, in_specs=ins, out_specs=out_specs, scratch_shapes=list(scratch)
         ),
         compiler_params=pltpu.CompilerParams(vmem_limit_bytes=limit << 20),
+        input_output_aliases=alias or {},
         cost_estimate=pl.CostEstimate(flops=flops, transcendentals=0, bytes_accessed=4 << 20),
     )
 
@@ -246,6 +247,25 @@
                 if b == 0:
                     o = o + carried[:, lanes]
                 out[rows, c * CH + k * 128 : c * CH + (k + 1) * 128] = o
+
+
+def back_local_when(which, core, og, wr, rd, run, *refs):
+    far_out, out, mid, sem = refs[-4:]
+
+    @pl.when(core[0] == which)
+    def _():
+        back_local_body(og, wr, rd, run, out, mid)
+        move = pltpu.make_async_copy(out, far_out, sem.at[0])
+        move.start()
+        move.wait()
+
+
+def back_local_early(*refs):
+    back_local_when(0, *refs)
+
+
+def back_local_late(*refs):
+    back_local_when(1, *refs)
 
 
 def places_body(ids, depth, count, camera, gain, asks, place_col, place_row, live, tile_gain):
@@ -416,7 +436,8 @@
             ends[2 * c + k] = end[:, k * 128 : (k + 1) * 128]
 
 
-def join_body(ends, mine, other, pay):
+def join_body(ends, mine, other, within, pay):
+    del within
     for g in range(OWN):
         pay[g, 0:NST, :] = ends[g]
         pay[g, NST : NST + HALF, :] = (mine[g].astype(F32) + other[g].astype(F32)).astype(BF16)
@@ -573,18 +594,32 @@
         [VMEM, VMEM],
         flops=1 << 31,
     )(held(low), head_weight, rd, held(run))
+    within_scratch = [
+        buf((TOK, WID), F32),
+        buf((NST, WID), BF16),
+        pltpu.SemaphoreType.DMA((1,)),
+    ]
+    (within,) = call(
+        back_local_early,
+        [((TOK, WID), F32, 1)],
+        [SMEM] + [VMEM] * 4,
+        [ANY],
+        scratch=within_scratch,
+        flops=1 << 32,
+    )(core_ref, held(out_grad), wr, rd, held(run))
     (pay,) = call(
-        join_body, [((OWN, NST + HALF, 128), BF16)], [VMEM] * 3, [VMEM]
-    )(held(back_ends), mine, other)
+        join_body, [((OWN, NST + HALF, 128), BF16)], [VMEM] * 3 + [ANY], [VMEM]
+    )(held(back_ends), mine, other, held(within))
     back = swap(pay, SEQ)
     (within,) = call(
-        back_local_body,
+        back_local_late,
         [((TOK, WID), F32, 1)],
-        [VMEM] * 4,
-        [VMEM],
-        scratch=[buf((NST, WID), BF16)],
+        [SMEM] + [VMEM] * 4 + [ANY],
+        [ANY],
+        scratch=within_scratch,
         flops=1 << 32,
-    )(held(out_grad), wr, rd, held(run))
+        alias={5: 0},
+    )(core_ref, held(out_grad), wr, rd, held(run), held(within))
     (part,) = call(scene_sum_body, [((HALF, 128), F32)], [VMEM], [VMEM])(back)
     part = (part + trade(part, 2)) + (trade(part, 4) + trade(part, 6))
     scale = np.float32(1.0 / np.sqrt(float(scenes * TOK * lax.axis_size(SEQ))))

time: 136 us -> 134 us (0.985)
  blocking collectives: 89.4 us -> 83.8 us
  waiting for transfers between devices: 5.41 us -> 8.54 us
    all_to_all x5, blocking collectives: 89.4 us -> 83.8 us  [swap(): return lax.all_to_all(x, axes, split_axis=0, concat_axis=0, tiled=True)]
    ppermute x5, waiting for transfers between devices: 1.51 us -> 4.63 us  [trade(): return lax.ppermute(v, 'dp', [(i, i ^ hop) for i in range(scenes)])]
    pallas_call x2 -> x3, Pallas kernels: 3.25 us -> 3.44 us  [the longest x1 3.31 us: shards(): call(back_local_early, [((TOK, WID), F32, 1)], [SMEM] + [VMEM] * 4, [ANY]...]
  transfers between devices with their start and end apart: 6 -> 6, of which waited for: 2 -> 3; matrix products, arithmetic and copies ran while one was open for 0% -> 0% of each run, Pallas kernels for 11% -> 11%
where the time goes in v4:
time: 134 us; the launch traced here: 132 us
  blocking collectives  83.8 us (63%)
  Pallas kernels  26.1 us (19%)
  starting transfers between devices  12.3 us (9%)
  waiting for transfers between devices  8.54 us (6%)
    all_to_all x5, blocking collectives, swap(): return lax.all_to_all(x, axes, split_axis=0, concat_axis=0, tiled=True)  83.8 us
    all_to_all x1, starting transfers between devices, swap(): return lax.all_to_all(x, axes, split_axis=0, concat_axis=0, tiled=True)  7.97 us
    pallas_call x1, Pallas kernels, shards(): call(fore_local_body, [((TOK, WID), F32, 0)], [VMEM] * 5, [VMEM], scratch...  5.59 us
    ppermute x5, waiting for transfers between devices, trade(): return lax.ppermute(v, 'dp', [(i, i ^ hop) for i in range(scenes)])  4.63 us
    ppermute x5, starting transfers between devices, trade(): return lax.ppermute(v, 'dp', [(i, i ^ hop) for i in range(scenes)])  4.34 us
    all_to_all x1, waiting for transfers between devices, swap(): return lax.all_to_all(x, axes, split_axis=0, concat_axis=0, tiled=True)  3.9 us
    pallas_call x1, Pallas kernels, shards(): call(back_local_early, [((TOK, WID), F32, 1)], [SMEM] + [VMEM] * 4, [ANY]...  3.31 us
    pallas_call x1, Pallas kernels, shards(): call(composite_body, [((OWN * 128, FEAT), BF16)], [VMEM] * 6, [VMEM], scr...  3.1 us
  transfers between devices with their start and end apart: 6, of which 3 were waited for; matrix products, arithmetic and copies ran while one was open for 0% of the time, Pallas kernels for 11%

profile of v4, /device:TPU:0, one launch (start us, length us, event | category | flops | bytes accessed | tf_op | source)
XLA Modules:
  0.0 131.8 jit_solution(13345508581211312351)
XLA Ops:
  0.7 3.0 %shard_map.131 = (bf16[16,136,128]{2,1,0:T(8,128)(2,1)}, f32[256,128]{1,0:T(8,128)S(1)}, f32[256,128]{1,0:T(8,128)S(1)}) custom-call(s32[1]{0:T(128)} %bitcast.core.refs_0_, bf16[256,2048]{1,0:T(8,128)(2,1)} %bitcast.35, bf16[256,128]{1,0:T(8,128)(2,1)} %bitcast.29, f32[64,256]{1,0:T(8,128)} %bitcast.46, f32[64,256]{1,0:T(8,128)} %bitcast.47), custom_call_target="tpu_custom_call" | custom-call | flops 536870912 | bytes 4194304 | tf_op jit(solution)/shard_map/pallas_call | solution.py:512
  3.7 8.0 %all-to-all-start = ((bf16[16,136,128]{2,1,0:T(8,128)(2,1)}), bf16[16,136,128]{2,1,0:T(8,128)(2,1)S(1)}, u32[]{:S(2)}, u32[]{:S(2)}) async-start(bf16[16,136,128]{2,1,0:T(8,128)(2,1)} %get-tuple-element.19), calls=%async_computation | async-start | bytes 1114112 | tf_op jit(solution)/shard_map/all_to_all | solution.py:486
  11.8 0.0 copy-start.1
  11.8 0.0 copy-start.2
  11.8 0.0 copy-start.5
  11.8 1.9 %shard_map.133 = (bf16[16,8,128]{2,1,0:T(8,128)(2,1)S(1)}, f32[1024,128]{1,0:T(8,128)}, f32[8,1024]{1,0:T(8,128)}, f32[64,16]{1,0:T(8,128)}, f32[64,256]{1,0:T(8,128)}) custom-call(s32[16,64]{1,0:T(8,128)S(1)} %bitcast.43, s32[16,64]{1,0:T(8,128)S(1)} %bitcast.44, s32[1,64]{1,0:T(1,128)S(1)} %copy-done.8, s32[1,64]{1,0:T(1,128)S(1)} %copy-done.9, ...), custom_call_target="tpu_custom_call" | custom-call | flops 2147483648 | bytes 4194304 | tf_op jit(solution)/shard_map/pallas_call | solution.py:527
  13.8 5.6 %shard_map.132.local = f32[256,2048]{1,0:T(8,128)} custom-call(bf16[256,2048]{1,0:T(8,128)(2,1)S(1)} %bitcast.36, bf16[256,128]{1,0:T(8,128)(2,1)S(1)} %bitcast.30, bf16[256,128]{1,0:T(8,128)(2,1)S(1)} %bitcast.38, f32[256,128]{1,0:T(8,128)S(1)} %get-tuple-element.17.run.refs_4_, f32[256,128]{1,0:T(8,128)S(1)} %get-tuple-element.18.step), custom_call_target="tpu_custom_call" | custom-call | flops 4294967296 | bytes 4194304 | tf_op jit(solution)/shard_map/pallas_call | solution.py:540
  19.4 3.9 %all-to-all-done.got.refs_1_ = bf16[16,136,128]{2,1,0:T(8,128)(2,1)S(1)} async-done(((bf16[16,136,128]{2,1,0:T(8,128)(2,1)}), bf16[16,136,128]{2,1,0:T(8,128)(2,1)S(1)}, u32[]{:S(2)}, u32[]{:S(2)}) %all-to-all-start) | async-done | bytes 557088 | tf_op jit(solution)/shard_map/all_to_all | solution.py:486
  23.3 0.1 shard_map.134
  23.4 14.8 %all_to_all.30.got.asked = bf16[16,136,128]{2,1,0:T(8,128)(2,1)S(1)} all-to-all(bf16[16,136,128]{2,1,0:T(8,128)(2,1)S(1)} %shard_map.134), channel_id=1, replica_groups=mesh['dp'=8,'seq_0'=4,'seq_1'=4] {'seq_0','seq_1'}, dimensions={0} | all-to-all | bytes 1114112 | tf_op jit(solution)/shard_map/all_to_all | solution.py:486
  38.2 1.8 %shard_map.135 = (bf16[256,2048]{1,0:T(8,128)(2,1)S(1)}, bf16[16,128,256]{2,1,0:T(8,128)(2,1)S(1)}) custom-call(f32[256,2048]{1,0:T(8,128)S(1)} %copy-done, bf16[16,136,128]{2,1,0:T(8,128)(2,1)S(1)} %all_to_all.30.got.asked, bf16[256,128]{1,0:T(8,128)(2,1)S(1)} %bitcast.39, f32[256,128]{1,0:T(8,128)S(1)} %get-tuple-element.17.run.refs_4_, ...), custom_call_target="tpu_custom_call" | custom-call | flops 2147483648 | bytes 4194304 | tf_op jit(solution)/shard_map/pallas_call | solution.py:552
  40.0 0.0 copy-start.4
  40.1 18.1 %all_to_all.31 = bf16[16,128,256]{2,1,0:T(8,128)(2,1)S(1)} all-to-all(bf16[16,128,256]{2,1,0:T(8,128)(2,1)S(1)} %get-tuple-element.21), channel_id=1, replica_groups=mesh['dp'=8,'seq_0'=4,'seq_1'=4] {'seq_0','seq_1'}, dimensions={0} | all-to-all | bytes 2097152 | tf_op jit(solution)/shard_map/all_to_all | solution.py:486
  58.2 3.1 %shard_map.136 = bf16[2048,256]{1,0:T(8,128)(2,1)S(1)} custom-call(bf16[2048,256]{1,0:T(8,128)(2,1)S(1)} %bitcast.27, f32[1024,128]{1,0:T(8,128)S(1)} %copy-done.10, f32[8,1024]{1,0:T(8,128)S(1)} %copy-done.12, f32[64,16]{1,0:T(8,128)S(1)} %copy-done.13, f32[64,256]{1,0:T(8,128)S(1)} %copy-done.11, f32[64,192]{1,0:T(8,128)S(1)} %bitcast.37), custom_call_target="tpu_custom_call" | custom-call | flops 4294967296 | bytes 4194304 | tf_op jit(solution)/shard_map/pallas_call | solution.py:560
  61.3 16.9 %all_to_all.32 = bf16[16,128,256]{2,1,0:T(8,128)(2,1)S(1)} all-to-all(bf16[16,128,256]{2,1,0:T(8,128)(2,1)S(1)} %bitcast.28), channel_id=1, replica_groups=mesh['dp'=8,'seq_0'=4,'seq_1'=4] {'seq_0','seq_1'}, dimensions={0} | all-to-all | bytes 2097152 | tf_op jit(solution)/shard_map/all_to_all | solution.py:486
  78.3 1.4 %shard_map.137 = (bf16[256,256]{1,0:T(8,128)(2,1)S(1)}, bf16[16,128,128]{2,1,0:T(8,128)(2,1)S(1)}, bf16[16,128,128]{2,1,0:T(8,128)(2,1)S(1)}) custom-call(s32[1]{0:T(128)} %bitcast.core.refs_0_, bf16[2048,256]{1,0:T(8,128)(2,1)S(1)} %bitcast.26, bf16[16,136,128]{2,1,0:T(8,128)(2,1)S(1)} %all_to_all.30.got.asked, bf16[256,2048]{1,0:T(8,128)(2,1)S(1)} %get-tuple-element.26.scan_out), custom_call_target="tpu_custom_call" | custom-call | flops 2147483648 | bytes 4194304 | tf_op jit(solution)/shard_map/pallas_call | solution.py:581
  79.7 0.1 collective-permute-start
  79.8 1.9 %shard_map.138 = (bf16[256,2048]{1,0:T(8,128)(2,1)S(1)}, bf16[16,128,128]{2,1,0:T(8,128)(2,1)S(1)}) custom-call(bf16[256,256]{1,0:T(8,128)(2,1)S(1)} %get-tuple-element.27.low, bf16[2048,256]{1,0:T(8,128)(2,1)S(1)} %copy-done.3, bf16[256,128]{1,0:T(8,128)(2,1)S(1)} %bitcast.40, f32[256,128]{1,0:T(8,128)S(1)} %get-tuple-element.17.run.refs_4_), custom_call_target="tpu_custom_call" | custom-call | flops 2147483648 | bytes 4194304 | tf_op jit(solution)/shard_map/pallas_call | solution.py:590
  81.7 3.3 %shard_map.139.refs_5_.within = f32[256,2048]{1,0:T(8,128)S(1)} custom-call(s32[1]{0:T(128)} %bitcast.core.refs_0_, bf16[256,2048]{1,0:T(8,128)(2,1)S(1)} %get-tuple-element.28.refs_1_, bf16[256,128]{1,0:T(8,128)(2,1)S(1)} %bitcast.31, bf16[256,128]{1,0:T(8,128)(2,1)S(1)} %bitcast.41, f32[256,128]{1,0:T(8,128)S(1)} %get-tuple-element.17.run.refs_4_), custom_call_target="tpu_custom_call" | custom-call | flops 4294967296 | bytes 4194304 | tf_op jit(solution)/shard_map/pallas_call | solution.py:602
  85.0 0.1 shard_map.141
  85.2 17.7 %all_to_all.33.got.refs_0_ = bf16[16,256,128]{2,1,0:T(8,128)(2,1)S(1)} all-to-all(bf16[16,256,128]{2,1,0:T(8,128)(2,1)S(1)} %shard_map.141), channel_id=1, replica_groups=mesh['dp'=8,'seq_0'=4,'seq_1'=4] {'seq_0','seq_1'}, dimensions={0} | all-to-all | bytes 2097152 | tf_op jit(solution)/shard_map/all_to_all | solution.py:486
  102.9 0.1 shard_map.142
  103.0 3.0 %collective-permute-start.3 = (f32[128,128]{1,0:T(8,128)S(1)}, f32[128,128]{1,0:T(8,128)S(1)}, u32[]{:S(2)}, u32[]{:S(2)}) collective-permute-start(f32[128,128]{1,0:T(8,128)S(1)} %shard_map.142), channel_id=1, source_target_pairs={{0,96},{16,112},{32,64},{48,80},{64,32},{80,48},{96,0},{112,16},{1... | collective-permute-start | bytes 196616 | tf_op jit(solution)/shard_map/ppermute | solution.py:510
  106.0 0.7 collective-permute-start.2
  106.7 0.4 collective-permute-start.1
  107.1 1.4 %collective-permute-done.3 = f32[128,128]{1,0:T(8,128)S(1)} collective-permute-done((f32[128,128]{1,0:T(8,128)S(1)}, f32[128,128]{1,0:T(8,128)S(1)}, u32[]{:S(2)}, u32[]{:S(2)}) %collective-permute-start.3) | collective-permute-done | bytes 65568 | tf_op jit(solution)/shard_map/ppermute | solution.py:510
  108.5 3.3 %collective-permute-done.2 = f32[128,128]{1,0:T(8,128)S(1)} collective-permute-done((f32[128,128]{1,0:T(8,128)S(1)}, f32[128,128]{1,0:T(8,128)S(1)}, u32[]{:S(2)}, u32[]{:S(2)}) %collective-permute-start.2) | collective-permute-done | bytes 65568 | tf_op jit(solution)/shard_map/ppermute | solution.py:510
  111.8 0.2 shard_map.143
  112.0 16.2 %all_to_all.34.got.own = bf16[16,256,128]{2,1,0:T(8,128)(2,1)S(1)} all-to-all(bf16[16,256,128]{2,1,0:T(8,128)(2,1)S(1)} %shard_map.143), channel_id=1, replica_groups=mesh['dp'=8,'seq_0'=4,'seq_1'=4] {'seq_0','seq_1'}, dimensions={0} | all-to-all | bytes 2097152 | tf_op jit(solution)/shard_map/all_to_all | solution.py:486
  128.3 0.1 collective-permute-start.4
  128.4 2.0 %shard_map.144 = bf16[256,2048]{1,0:T(8,128)(2,1)} custom-call(f32[256,2048]{1,0:T(8,128)S(1)} %shard_map.140.refs_3_.within, bf16[16,256,128]{2,1,0:T(8,128)(2,1)S(1)} %all_to_all.34.got.own, bf16[256,128]{1,0:T(8,128)(2,1)S(1)} %bitcast.33, f32[256,128]{1,0:T(8,128)S(1)} %get-tuple-element.17.run.refs_4_, f32[256,128]{1,0:T(8,128)S(1)} %get-tuple-element.18.step), custom_call_target="tpu_custom_call" | custom-call | flops 1073741824 | bytes 4194304 | tf_op jit(solution)/shard_map/pallas_call | solution.py:635
  130.3 1.5 %shard_map.145 = f32[2048,256]{1,0:T(8,128)} custom-call(s32[1]{0:T(128)} %bitcast.core.refs_0_, bf16[16,256,128]{2,1,0:T(8,128)(2,1)S(1)} %all_to_all.34.got.own, bf16[16,128,128]{2,1,0:T(8,128)(2,1)S(1)} %collective-permute-done.4.other), custom_call_target="tpu_custom_call" | custom-call | bytes 4194304 | tf_op jit(solution)/shard_map/pallas_call | solution.py:638
  (33 shorter events, 0.1 us)
Async XLA Ops:
  0.6 11.1 %copy-start.14 = (f32[1,8,3]{1,0,2:T(1,128)S(1)}, f32[1,8,3]{1,0,2:T(1,128)}, u32[]{:S(2)}) copy-start(f32[1,8,3]{1,0,2:T(1,128)} %param.22) | copy-start | bytes 292
  0.6 11.1 %copy-start.9 = (s32[1,64]{1,0:T(1,128)S(1)}, s32[1,64]{1,0:T(1,128)}, u32[]{:S(2)}) copy-start(s32[1,64]{1,0:T(1,128)} %camera.1) | copy-start | bytes 772
  0.7 11.1 %copy-start.7 = (s32[1,64,16]{1,2,0:T(8,128)S(1)}, s32[1,64,16]{1,2,0:T(8,128)}, u32[]{:S(2)}) copy-start(s32[1,64,16]{1,2,0:T(8,128)} %param.20) | copy-start | bytes 12292
  0.7 11.1 %copy-start.8 = (s32[1,64]{1,0:T(1,128)S(1)}, s32[1,64]{1,0:T(1,128)}, u32[]{:S(2)}) copy-start(s32[1,64]{1,0:T(1,128)} %count.1) | copy-start | bytes 772
  0.7 11.1 %copy-start.6 = (s32[1,64,16]{1,2,0:T(8,128)S(1)}, s32[1,64,16]{1,2,0:T(8,128)}, u32[]{:S(2)}) copy-start(s32[1,64,16]{1,2,0:T(8,128)} %param.18) | copy-start | bytes 12292
  3.7 19.5 %all-to-all-start = ((bf16[16,136,128]{2,1,0:T(8,128)(2,1)}), bf16[16,136,128]{2,1,0:T(8,128)(2,1)S(1)}, u32[]{:S(2)}, u32[]{:S(2)}) async-start(bf16[16,136,128]{2,1,0:T(8,128)(2,1)} %get-tuple-element.19), calls=%async_computation | async-start | bytes 1114112 | tf_op jit(solution)/shard_map/all_to_all | solution.py:486
  11.8 2.0 %copy-start.1 = (bf16[1,256,128]{2,1,0:T(8,128)(2,1)S(1)}, bf16[1,256,128]{2,1,0:T(8,128)(2,1)}, u32[]{:S(2)}) copy-start(bf16[1,256,128]{2,1,0:T(8,128)(2,1)} %param.13) | copy-start | bytes 196612
  11.8 2.0 %copy-start.2 = (bf16[1,256,2048]{2,1,0:T(8,128)(2,1)S(1)}, bf16[1,256,2048]{2,1,0:T(8,128)(2,1)}, u32[]{:S(2)}) copy-start(bf16[1,256,2048]{2,1,0:T(8,128)(2,1)} %param.12) | copy-start | bytes 3145732
  11.8 2.0 %copy-start.5 = (bf16[1,256,128]{2,1,0:T(8,128)(2,1)S(1)}, bf16[1,256,128]{2,1,0:T(8,128)(2,1)}, u32[]{:S(2)}) copy-start(bf16[1,256,128]{2,1,0:T(8,128)(2,1)} %param.14) | copy-start | bytes 196612
  23.3 15.0 %copy-start = (f32[256,2048]{1,0:T(8,128)S(1)}, f32[256,2048]{1,0:T(8,128)}, u32[]{:S(2)}) copy-start(f32[256,2048]{1,0:T(8,128)} %shard_map.132.local) | copy-start | bytes 6291460
  23.3 15.0 %copy-start.3 = (bf16[2048,256]{1,0:T(8,128)(2,1)S(1)}, bf16[2048,256]{1,0:T(8,128)(2,1)}, u32[]{:S(2)}) copy-start(bf16[2048,256]{1,0:T(8,128)(2,1)} %weight.3) | copy-start | bytes 3145732
  40.0 18.2 %copy-start.4 = (f32[1,64,192]{2,1,0:T(8,128)S(1)}, f32[1,64,192]{2,1,0:T(8,128)}, u32[]{:S(2)}) copy-start(f32[1,64,192]{2,1,0:T(8,128)} %param.23) | copy-start | bytes 147460
  40.1 18.1 %copy-start.10 = (f32[1024,128]{1,0:T(8,128)S(1)}, f32[1024,128]{1,0:T(8,128)}, u32[]{:S(2)}) copy-start(f32[1024,128]{1,0:T(8,128)} %get-tuple-element.22.place_col) | copy-start | bytes 1572868
  40.1 18.1 %copy-start.11 = (f32[64,256]{1,0:T(8,128)S(1)}, f32[64,256]{1,0:T(8,128)}, u32[]{:S(2)}) copy-start(f32[64,256]{1,0:T(8,128)} %get-tuple-element.25.tile_gain) | copy-start | bytes 196612
  40.1 18.1 %copy-start.12 = (f32[8,1024]{1,0:T(8,128)S(1)}, f32[8,1024]{1,0:T(8,128)}, u32[]{:S(2)}) copy-start(f32[8,1024]{1,0:T(8,128)} %get-tuple-element.23.place_row) | copy-start | bytes 98308
  40.1 18.1 %copy-start.13 = (f32[64,16]{1,0:T(8,128)S(1)}, f32[64,16]{1,0:T(8,128)}, u32[]{:S(2)}) copy-start(f32[64,16]{1,0:T(8,128)} %get-tuple-element.24.live) | copy-start | bytes 12292
  79.7 5.3 %collective-permute-start = (bf16[16,128,128]{2,1,0:T(8,128)(2,1)S(1)}, bf16[16,128,128]{2,1,0:T(8,128)(2,1)S(1)}, u32[]{:S(2)}, u32[]{:S(2)}) collective-permute-start(bf16[16,128,128]{2,1,0:T(8,128)(2,1)S(1)} %get-tuple-element.31), channel_id=1, source_target_pairs={{0,16},{16,0},{32,48},{48,32},{64,80},{80,64},{96,112},{112,96},{1... | collective-permute-start | bytes 1572872 | tf_op jit(solution)/shard_map/ppermute | solution.py:510
  103.0 5.6 %collective-permute-start.3 = (f32[128,128]{1,0:T(8,128)S(1)}, f32[128,128]{1,0:T(8,128)S(1)}, u32[]{:S(2)}, u32[]{:S(2)}) collective-permute-start(f32[128,128]{1,0:T(8,128)S(1)} %shard_map.142), channel_id=1, source_target_pairs={{0,96},{16,112},{32,64},{48,80},{64,32},{80,48},{96,0},{112,16},{1... | collective-permute-start | bytes 196616 | tf_op jit(solution)/shard_map/ppermute | solution.py:510
  106.0 5.8 %collective-permute-start.2 = (f32[128,128]{1,0:T(8,128)S(1)}, f32[128,128]{1,0:T(8,128)S(1)}, u32[]{:S(2)}, u32[]{:S(2)}) collective-permute-start(f32[128,128]{1,0:T(8,128)S(1)} %shard_map.142), channel_id=1, source_target_pairs={{0,64},{16,80},{32,96},{48,112},{64,0},{80,16},{96,32},{112,48},{1... | collective-permute-start | bytes 196616 | tf_op jit(solution)/shard_map/ppermute | solution.py:510
  106.7 5.1 %collective-permute-start.1 = (f32[128,128]{1,0:T(8,128)S(1)}, f32[128,128]{1,0:T(8,128)S(1)}, u32[]{:S(2)}, u32[]{:S(2)}) collective-permute-start(f32[128,128]{1,0:T(8,128)S(1)} %shard_map.142), channel_id=1, source_target_pairs={{0,32},{16,48},{32,0},{48,16},{64,96},{80,112},{96,64},{112,80},{1... | collective-permute-start | bytes 196616 | tf_op jit(solution)/shard_map/ppermute | solution.py:510
  128.3 2.1 %collective-permute-start.4 = (bf16[16,128,128]{2,1,0:T(8,128)(2,1)S(1)}, bf16[16,128,128]{2,1,0:T(8,128)(2,1)S(1)}, u32[]{:S(2)}, u32[]{:S(2)}) collective-permute-start(bf16[16,128,128]{2,1,0:T(8,128)(2,1)S(1)} %slice.4), channel_id=1, source_target_pairs={{0,16},{16,0},{32,48},{48,32},{64,80},{80,64},{96,112},{112,96},{1... | collective-permute-start | bytes 1572872 | tf_op jit(solution)/shard_map/ppermute | solution.py:510
